TPU v7x, 256 devices: a whole 4x4x8 slice. The times are simulated.
256 devices in a mesh: gz: 64 (over z, x, y_hi), gx: 2 (over core), gy: 2 (over y_lo).
Axes of the slice: x: 4, y: 4 (y_hi: 2, y_lo: 2; y = y_hi * 2 + y_lo), z: 8, core: 2. Of those that a mesh axis runs over, the one named last changes fastest.
Arguments:
- rhs_field: float32 [128, 8, 8, 512], P('gz', 'gy', 'gx'), may hold values from -1 to 1
- start_field: float32 [128, 8, 8, 512], P('gz', 'gy', 'gx'), may hold values from -0.2 to 0.2
- material: int32 [128, 8, 8], P('gz', 'gy', 'gx'), may hold values from 0 to 3
- diag_inverse: float32 [4, 64, 64], replicated, may hold values from -0.2 to 0.2
- z_blocks: float32 [4, 2, 64, 64], replicated, may hold values from -10 to 10
- side_blocks: float32 [4, 4, 64, 64], replicated, may hold values from -0.375 to 0.375
Outputs:
- forward_field: float32 [128, 8, 8, 512], P('gz', 'gy', 'gx')
- backward_field: float32 [128, 8, 8, 512], P('gz', 'gy', 'gx')
Inputs may be any that keep to these rules, and one draw needn't show every extreme that they name: material[e] selects the element's tables.
All inputs are finite; a program needn't handle non-finite values.
Results may differ from a plain program's by a relative error of at most 0.0003.
Values sent between devices are 32-bit elements; how exact they have to be, the bound alone decides.
No kernel may reach another device: no remote copies, remote signals or barrier semaphores. Data moves between devices by JAX's collectives and lax.ppermute only.
A program may use at most 128 MiB of HBM per device.

v0:
```python
import functools

import jax
import jax.numpy as jnp
from jax import lax
from jax.experimental import pallas as pl
from jax.experimental.pallas import tpu as pltpu
from jax.sharding import Mesh
from jax.sharding import PartitionSpec as P

GZ = ("ah", "am", "al", "b", "c")
HIGH = lax.Precision.HIGHEST
F32 = jnp.float32
BF16 = jnp.bfloat16

LANES = 128
DOFS = 64
KINDS = 4
STEPS = 8
CHUNKS = 16
ROWS = STEPS * CHUNKS
PEERS = 64
SLOTS = 6
VMEM = pl.BlockSpec(memory_space=pltpu.VMEM)
SMEM = pl.BlockSpec(memory_space=pltpu.SMEM)


def split(value):
    high = value.astype(BF16)
    return high, (value - high.astype(F32)).astype(BF16)


def doubled(pairs):
    low = lax.broadcasted_iota(jnp.int32, pairs.shape, 1) < DOFS
    turned = pltpu.roll(pairs, DOFS, 1)
    return jnp.concatenate([jnp.where(low, pairs, turned), jnp.where(low, turned, pairs)], axis=0)


def fold(product):
    rows = product.shape[0] // 2
    top, bottom = product[:rows], product[rows:]
    return (top[:, :LANES] + top[:, LANES:]) + (bottom[:, :LANES] + bottom[:, LANES:])


def widened(value, mask_a, mask_b):
    high, low = split(value)
    return jnp.concatenate(
        [
            jnp.concatenate([high * mask_a, high * mask_b], axis=1),
            jnp.concatenate([low * mask_a, low * mask_b], axis=1),
        ],
        axis=0,
    )


def block_of(y, x, flip_y, flip_x):
    return (y ^ flip_y) * 8 + (x ^ flip_x) * 2


def pack_kernel(where_ref, mat_ref, rhs_ref, start_ref, out_ref):
    flip_x, flip_y = where_ref[0], where_ref[1]
    for y in range(4):
        for x in range(4):
            block = block_of(y, x, flip_y, flip_x)
            cell = y * 4 + x
            for p in range(2):
                kind = jnp.full((1, LANES), mat_ref[p, cell].astype(F32))
                for part in range(4):
                    lanes = slice(part * LANES, (part + 1) * LANES)
                    slot = block + (part // 2) * 32 + part % 2
                    out_ref[slot, p : p + 1, :] = rhs_ref[p, cell : cell + 1, lanes]
                    out_ref[slot, 2 + p : 3 + p, :] = start_ref[p, cell : cell + 1, lanes]
                    out_ref[slot, 4 + p : 5 + p, :] = kind


def unpack_kernel(where_ref, in_ref, forward_ref, backward_ref):
    flip_x, flip_y = where_ref[0], where_ref[1]
    for y in range(4):
        for x in range(4):
            block = block_of(y, x, flip_y, flip_x)
            cell = y * 4 + x
            for part in range(4):
                lanes = slice(part * LANES, (part + 1) * LANES)
                slot = block + (part // 2) * 32 + part % 2
                for p in range(2):
                    forward_ref[p, cell : cell + 1, lanes] = in_ref[slot, p : p + 1, :]
                    backward_ref[p, cell : cell + 1, lanes] = in_ref[slot, 2 + p : 3 + p, :]


def arrange_kernel(in_ref, rhs_ref, start_ref, kind_ref):
    for step in range(STEPS):
        for chunk in range(CHUNKS):
            block, p = chunk * 4 + step // 2, step % 2
            row = step * CHUNKS + chunk
            rhs_ref[row : row + 1, :] = in_ref[block, p : p + 1, :]
            start_ref[row : row + 1, :] = in_ref[block, 2 + p : 3 + p, :]
            kind_ref[row : row + 1, :] = in_ref[block, 4 + p : 5 + p, :]


def masks_of(kind):
    half = (lax.broadcasted_iota(jnp.int32, kind.shape, 1) >= DOFS).astype(F32)
    mask_a = jnp.where(kind == half, 1.0, 0.0).astype(BF16)
    mask_b = jnp.where(kind == half + 2.0, 1.0, 0.0).astype(BF16)
    return mask_a, mask_b


def tables_kernel(diag_ref, z_ref, side_ref, kind_ref, tables_ref, mask_a_ref, mask_b_ref, map_f_ref, map_b_ref,
                  plain_ref, run_ref, wide_ref):
    for m in range(KINDS):
        inverse = jnp.concatenate([diag_ref[m], diag_ref[m]], axis=1)
        left = jnp.concatenate([z_ref[m].reshape(2 * DOFS, DOFS), side_ref[m].reshape(4 * DOFS, DOFS)], axis=0)
        joined = jnp.dot(left, inverse, precision=HIGH, preferred_element_type=F32)
        joined = jnp.concatenate([joined, inverse], axis=0)
        high, low = split(joined)
        for q in range(7):
            rows = slice(q * DOFS, (q + 1) * DOFS)
            tables_ref[q, m * DOFS : (m + 1) * DOFS, :LANES] = high[rows]
            tables_ref[q, m * DOFS : (m + 1) * DOFS, LANES:] = low[rows]
        for q in range(2):
            plain_ref[q, m] = joined[q * DOFS : (q + 1) * DOFS]
    mask_a, mask_b = masks_of(kind_ref[...])
    mask_a_ref[...] = mask_a
    mask_b_ref[...] = mask_b

    for q, map_ref in ((0, map_f_ref), (1, map_b_ref)):
        order = list(range(STEPS)) if q == 0 else list(reversed(range(STEPS)))
        for chunk in range(CHUNKS):
            row = order[0] * CHUNKS + chunk
            kind = jnp.broadcast_to(kind_ref[row : row + 1, :], (DOFS, LANES))
            first = jnp.where(kind == 0.0, plain_ref[q, 0], plain_ref[q, 1])
            second = jnp.where(kind == 2.0, plain_ref[q, 2], plain_ref[q, 3])
            run_ref[chunk] = jnp.where(kind < 2.0, first, second)
        for step in order[1:]:
            for group in range(4):
                for k in range(4):
                    chunk = group * 4 + k
                    row = step * CHUNKS + chunk
                    a = jnp.broadcast_to(mask_a[row : row + 1, :], (DOFS, LANES))
                    b = jnp.broadcast_to(mask_b[row : row + 1, :], (DOFS, LANES))
                    wide_ref[k * 2 * DOFS : (k + 1) * 2 * DOFS, :] = widened(run_ref[chunk], a, b)
                product = jnp.dot(wide_ref[...], tables_ref[q], preferred_element_type=F32)
                for k in range(4):
                    run_ref[group * 4 + k] = fold(product[k * 2 * DOFS : (k + 1) * 2 * DOFS])
        for chunk in range(CHUNKS):
            high, low = split(run_ref[chunk])
            map_ref[chunk, :DOFS, :] = high
            map_ref[chunk, DOFS:, :] = low


def chain(const_ref, mask_a_ref, mask_b_ref, table_ref, map_ref, ends_ref, heads_ref, out_ref, descending):
    steps = list(range(STEPS))
    chunks = list(range(CHUNKS))
    if descending:
        steps, chunks = steps[::-1], chunks[::-1]

    def known(step):
        rows = pl.ds(step * CHUNKS, CHUNKS)
        return jnp.concatenate([const_ref[rows, :], const_ref[pl.ds(ROWS + step * CHUNKS, CHUNKS), :]], axis=0)

    def advance(state, step):
        rows = pl.ds(step * CHUNKS, CHUNKS)
        a, b = mask_a_ref[rows, :], mask_b_ref[rows, :]
        wide = widened(state, jnp.concatenate([a, a], axis=0), jnp.concatenate([b, b], axis=0))
        product = jnp.dot(wide, table_ref[...], preferred_element_type=F32)
        return known(step) - fold(product)

    state = known(steps[0])
    for step in steps[1:]:
        state = advance(state, step)
    ends_ref[...] = state

    row = lax.broadcasted_iota(jnp.int32, (8, LANES), 0)
    second = (row & 1) == 1
    rest = (row & 2) == 2
    head = jnp.zeros((8, LANES), F32)
    for chunk in chunks:
        heads_ref[chunk : chunk + 1, :] = head[0:1]
        heads_ref[CHUNKS + chunk : CHUNKS + chunk + 1, :] = head[1:2]
        if chunk == chunks[-1]:
            break
        high = head.astype(BF16).astype(F32)
        wide = jnp.where(rest, head - high, high).astype(BF16)
        product = jnp.dot(wide, map_ref[chunk], preferred_element_type=F32)
        ends = jnp.where(
            second,
            jnp.broadcast_to(ends_ref[CHUNKS + chunk : CHUNKS + chunk + 1, :], (8, LANES)),
            jnp.broadcast_to(ends_ref[chunk : chunk + 1, :], (8, LANES)),
        )
        head = (product + pltpu.roll(product, 2, 0)) + ends

    low = lax.broadcasted_iota(jnp.int32, (CHUNKS, LANES), 1) < DOFS
    state = heads_ref[...]
    for step in steps:
        state = advance(state, step)
        out_ref[pl.ds(step * CHUNKS, CHUNKS), :] = jnp.where(low, state[:CHUNKS], state[CHUNKS:])


def neighbour_terms(wide_ref, pieces, mask_a, mask_b, tables_ref, first):
    for k, piece in enumerate(pieces):
        wide_ref[:, k * 256 : (k + 1) * 256] = widened(doubled(piece), mask_a, mask_b)
    total = None
    for k in range(len(pieces)):
        product = jnp.dot(wide_ref[:, k * 256 : (k + 1) * 256], tables_ref[first + k], preferred_element_type=F32)
        total = product if total is None else total + product
    return fold(total)


def both(mask):
    return jnp.concatenate([mask, mask], axis=0)


def forward_kernel(edge_ref, rhs_ref, start_ref, n0_ref, n1_ref, n2_ref, n3_ref, mask_a_ref, mask_b_ref, tables_ref,
                   map_ref, forward_ref, given_ref, const_ref, ends_ref, heads_ref, wide_ref):
    mask_a, mask_b = both(mask_a_ref[...]), both(mask_b_ref[...])
    start = start_ref[...]
    following = jnp.concatenate([start[1:CHUNKS], jnp.zeros((1, LANES), F32)], axis=0)
    upper = jnp.concatenate([start[CHUNKS:], following], axis=0)
    pieces = [upper]
    for k, ref in enumerate((n0_ref, n1_ref, n2_ref, n3_ref)):
        pieces.append(jnp.where(edge_ref[k] > 0, ref[...], 0.0))
    given = neighbour_terms(wide_ref, pieces, mask_a, mask_b, tables_ref, 1)
    given_ref[...] = given
    own = widened(doubled(rhs_ref[...]), mask_a, mask_b)
    const_ref[...] = fold(jnp.dot(own, tables_ref[6], preferred_element_type=F32)) - given
    chain(const_ref, mask_a_ref, mask_b_ref, tables_ref.at[0], map_ref, ends_ref, heads_ref, forward_ref, False)


def backward_kernel(edge_ref, forward_ref, given_ref, n0_ref, n1_ref, n2_ref, n3_ref, mask_a_ref, mask_b_ref,
                    tables_ref, map_ref, out_ref, const_ref, ends_ref, heads_ref, wide_ref, backward_ref):
    mask_a, mask_b = both(mask_a_ref[...]), both(mask_b_ref[...])
    pieces = []
    for k, ref in enumerate((n0_ref, n1_ref, n2_ref, n3_ref)):
        pieces.append(jnp.where(edge_ref[k] > 0, ref[...], 0.0))
    terms = neighbour_terms(wide_ref, pieces, mask_a, mask_b, tables_ref, 2)
    const_ref[...] = doubled(forward_ref[...]) + (given_ref[...] - terms)
    chain(const_ref, mask_a_ref, mask_b_ref, tables_ref.at[1], map_ref, ends_ref, heads_ref, backward_ref, True)
    for step in range(STEPS):
        for chunk in range(CHUNKS):
            block, p = chunk * 4 + step // 2, step % 2
            row = step * CHUNKS + chunk
            out_ref[block, p : p + 1, :] = forward_ref[row : row + 1, :]
            out_ref[block, 2 + p : 3 + p, :] = backward_ref[row : row + 1, :]
    for block in range(PEERS):
        out_ref[block, 4:6, :] = jnp.zeros((2, LANES), F32)


def shape(*dims, dtype=F32):
    return jax.ShapeDtypeStruct(dims, dtype)


def call(kernel, outs, ins, scratch=(), flops=1000000):
    return pl.pallas_call(
        kernel,
        out_shape=outs,
        in_specs=ins,
        out_specs=jax.tree.map(lambda _: VMEM, outs),
        scratch_shapes=scratch,
        cost_estimate=pl.CostEstimate(flops=flops, bytes_accessed=500000, transcendentals=0),
    )


X_AXES, Y_AXES = ("b", "gx"), ("am", "al", "gy")
RING = [0, 2, 4, 6, 7, 5, 3, 1]


def moved(value, axes, distance):
    pairs = [(RING[i], RING[(i + distance) % 8]) for i in range(8)]
    return lax.ppermute(value, axes, pairs)


def neighbours(value):
    return [
        moved(value, Y_AXES, 1),
        moved(value, Y_AXES, -1),
        moved(value, X_AXES, 1),
        moved(value, X_AXES, -1),
    ]


def per_device(rhs_field, start_field, material, diag_inverse, z_blocks, side_blocks):
    gx, gy = lax.axis_index("gx"), lax.axis_index("gy")
    where = jnp.stack([gx * 3, gy * 3]).astype(jnp.int32)
    x = lax.axis_index("b")
    y = lax.axis_index("am") * 2 + lax.axis_index("al")
    x = jnp.where(gx == 1, 7 - x, x)
    y = jnp.where(gy == 1, 7 - y, y)
    edge = jnp.stack([y > 0, y < 7, x > 0, x < 7]).astype(jnp.int32)

    packed = call(pack_kernel, shape(PEERS, SLOTS, LANES), [SMEM, SMEM, VMEM, VMEM])(
        where, material.reshape(2, 16), rhs_field.reshape(2, 16, 512), start_field.reshape(2, 16, 512)
    )
    arrived = lax.all_to_all(packed, GZ, 0, 0, tiled=True)
    rhs, start, kind = call(
        arrange_kernel, (shape(ROWS, LANES), shape(ROWS, LANES), shape(ROWS, LANES)), [VMEM]
    )(arrived)
    beside = neighbours(start)

    maps = shape(CHUNKS, 2 * DOFS, LANES, dtype=BF16)
    mask = shape(ROWS, LANES, dtype=BF16)
    tables, mask_a, mask_b, map_f, map_b = call(
        tables_kernel,
        (shape(7, 256, 256, dtype=BF16), mask, mask, maps, maps),
        [VMEM] * 4,
        [
            pltpu.VMEM((2, KINDS, DOFS, LANES), F32),
            pltpu.VMEM((CHUNKS, DOFS, LANES), F32),
            pltpu.VMEM((8 * DOFS, 256), BF16),
        ],
        flops=4000000000,
    )(diag_inverse, z_blocks, side_blocks, kind)

    chain_scratch = [
        pltpu.VMEM((2 * ROWS, LANES), F32),
        pltpu.VMEM((2 * CHUNKS, LANES), F32),
        pltpu.VMEM((2 * CHUNKS, LANES), F32),
    ]
    forward, given = call(
        forward_kernel,
        (shape(ROWS, LANES), shape(2 * ROWS, LANES)),
        [SMEM] + [VMEM] * 10,
        chain_scratch + [pltpu.VMEM((4 * ROWS, 5 * 256), BF16)],
        flops=4000000000,
    )(edge, rhs, start, *beside, mask_a, mask_b, tables, map_f)

    beside = neighbours(forward)
    ready = call(
        backward_kernel,
        shape(PEERS, SLOTS, LANES),
        [SMEM] + [VMEM] * 10,
        chain_scratch + [pltpu.VMEM((4 * ROWS, 4 * 256), BF16), pltpu.VMEM((ROWS, LANES), F32)],
        flops=4000000000,
    )(edge, forward, given, *beside, mask_a, mask_b, tables, map_b)
    returned = lax.all_to_all(ready, GZ, 0, 0, tiled=True)
    out_f, out_b = call(unpack_kernel, (shape(2, 16, 512), shape(2, 16, 512)), [SMEM, VMEM])(where, returned)
    return out_f.reshape(rhs_field.shape), out_b.reshape(rhs_field.shape)


def solution(mesh):
    finer = Mesh(
        mesh.devices.reshape(2, 2, 2, 4, 2, mesh.shape["gx"], mesh.shape["gy"]),
        GZ + ("gx", "gy"),
    )
    placed = (P(GZ, "gy", "gx", None), P(GZ, "gy", "gx", None), P(GZ, "gy", "gx"), P(), P(), P())
    return jax.shard_map(
        per_device,
        mesh=finer,
        in_specs=placed,
        out_specs=(P(GZ, "gy", "gx", None), P(GZ, "gy", "gx", None)),
        check_vma=False,
    )
```

profile of v0, /device:TPU:2, one launch (start us, length us, event | category | flops | bytes accessed | tf_op | source)
XLA Modules:
  0.0 92.8 jit_solution(17606330374505875264)
XLA Ops:
  0.6 0.7 copy-done.3
  1.9 1.5 %reshape.20.rhs_ref = f32[2,16,512]{2,1,0:T(8,128)} reshape(f32[2,4,4,512]{3,2,1,0:T(4,128)} %param.6) | data formatting | bytes 131072 | tf_op jit(solution)/shard_map/reshape | solution.py:290
  3.5 0.7 reshape.21.start_ref
  4.1 0.6 pad_add_fusion.where_ref
  4.8 1.7 %shard_map.77 = f32[64,6,128]{2,1,0:T(8,128)} custom-call(s32[2]{0:T(128)} %pad_add_fusion.where_ref, s32[2,16]{1,0:T(2,128)} %reshape.19.mat_ref, f32[2,16,512]{2,1,0:T(8,128)} %reshape.20.rhs_ref, f32[2,16,512]{2,1,0:T(8,128)} %reshape.21.start_ref), custom_call_target="tpu_custom_call" | custom-call | flops 1000000 | bytes 500000 | tf_op jit(solution)/shard_map/pallas_call | solution.py:289
  6.5 14.6 %all-to-all-start = ((f32[64,6,128]{2,1,0:T(8,128)}), f32[64,6,128]{2,1,0:T(8,128)S(1)}, u32[]{:S(2)}, u32[]{:S(2)}) async-start(f32[64,6,128]{2,1,0:T(8,128)} %shard_map.77), calls=%async_computation | async-start | bytes 524288 | tf_op jit(solution)/shard_map/all_to_all | solution.py:292
  21.8 12.8 %all-to-all-done.in_ref = f32[64,6,128]{2,1,0:T(8,128)S(1)} async-done(((f32[64,6,128]{2,1,0:T(8,128)}), f32[64,6,128]{2,1,0:T(8,128)S(1)}, u32[]{:S(2)}, u32[]{:S(2)}) %all-to-all-start) | async-done | bytes 196640 | tf_op jit(solution)/shard_map/all_to_all | solution.py:292
  34.5 0.7 copy-done
  35.2 1.8 %shard_map.78 = (f32[128,128]{1,0:T(8,128)}, f32[128,128]{1,0:T(8,128)}, f32[128,128]{1,0:T(8,128)}) custom-call(f32[64,6,128]{2,1,0:T(8,128)} %copy-done), custom_call_target="tpu_custom_call" | custom-call | flops 1000000 | bytes 500000 | tf_op jit(solution)/shard_map/pallas_call | solution.py:293
  37.0 1.5 %collective-permute-start.3 = (f32[128,128]{1,0:T(8,128)}, f32[128,128]{1,0:T(8,128)S(1)}, u32[]{:S(2)}, u32[]{:S(2)}) collective-permute-start(f32[128,128]{1,0:T(8,128)} %get-tuple-element.15.start_ref), channel_id=1, source_target_pairs={{0,2},{8,0},{16,8},{24,16},{26,24},{18,26},{10,18},{2,10},{1,3},{9... | collective-permute-start | bytes 196616 | tf_op jit(solution)/shard_map/ppermute | solution.py:268
  39.0 0.7 collective-permute-start.1
  39.7 1.3 %collective-permute-start = (f32[128,128]{1,0:T(8,128)}, f32[128,128]{1,0:T(8,128)S(1)}, u32[]{:S(2)}, u32[]{:S(2)}) collective-permute-start(f32[128,128]{1,0:T(8,128)} %get-tuple-element.15.start_ref), channel_id=1, source_target_pairs={{0,32},{32,64},{64,96},{96,97},{97,65},{65,33},{33,1},{1,0},{2,34}... | collective-permute-start | bytes 196616 | tf_op jit(solution)/shard_map/ppermute | solution.py:268
  41.0 6.8 %shard_map.79 = (bf16[7,256,256]{2,1,0:T(8,128)(2,1)}, bf16[128,128]{1,0:T(8,128)(2,1)}, bf16[128,128]{1,0:T(8,128)(2,1)}, bf16[16,128,128]{2,1,0:T(8,128)(2,1)}, bf16[16,128,128]{2,1,0:T(8,128)(2,1)}) custom-call(f32[4,64,64]{2,1,0:T(8,128)} %diag_ref.1, f32[4,2,64,64]{3,2,1,0:T(8,128)} %z_ref.1, f32[4,4,64,64]{3,2,1,0:T(8,128)} %side_ref.1, ...), custom_call_target="tpu_custom_call" | custom-call | flops 4000000000 | bytes 500000 | tf_op jit(solution)/shard_map/pallas_call | solution.py:300
  48.5 6.7 %shard_map.80 = (f32[128,128]{1,0:T(8,128)}, f32[256,128]{1,0:T(8,128)}) custom-call(s32[4]{0:T(128)} %add_convert_fusion.edge_ref, f32[128,128]{1,0:T(8,128)} %get-tuple-element.14.rhs_ref, f32[128,128]{1,0:T(8,128)} %get-tuple-element.15.start_ref, f32[128,128]{1,0:T(8,128)} %copy-done.9, f32[128,128]{1,0:T(8,128)} %copy-done.7, f32[128,128]{1,0:T(8,128)} %copy-done.5, ...), custom_call_target="tpu_custom_call" | custom-call | flops 4000000000 | bytes 500000 | tf_op jit(solution)/shard_map/pallas_call | solution.py:317
  55.2 1.5 %collective-permute-start.7 = (f32[128,128]{1,0:T(8,128)}, f32[128,128]{1,0:T(8,128)S(1)}, u32[]{:S(2)}, u32[]{:S(2)}) collective-permute-start(f32[128,128]{1,0:T(8,128)} %get-tuple-element.21.forward_ref), channel_id=1, source_target_pairs={{0,2},{8,0},{16,8},{24,16},{26,24},{18,26},{10,18},{2,10},{1,3},{9... | collective-permute-start | bytes 196616 | tf_op jit(solution)/shard_map/ppermute | solution.py:268
  57.3 0.7 collective-permute-start.5
  57.9 1.3 %collective-permute-start.4 = (f32[128,128]{1,0:T(8,128)}, f32[128,128]{1,0:T(8,128)S(1)}, u32[]{:S(2)}, u32[]{:S(2)}) collective-permute-start(f32[128,128]{1,0:T(8,128)} %get-tuple-element.21.forward_ref), channel_id=1, source_target_pairs={{0,32},{32,64},{64,96},{96,97},{97,65},{65,33},{33,1},{1,0},{2,34}... | collective-permute-start | bytes 196616 | tf_op jit(solution)/shard_map/ppermute | solution.py:268
  59.7 1.5 %collective-permute-done.6.n2_ref = f32[128,128]{1,0:T(8,128)S(1)} collective-permute-done((f32[128,128]{1,0:T(8,128)}, f32[128,128]{1,0:T(8,128)S(1)}, u32[]{:S(2)}, u32[]{:S(2)}) %collective-permute-start.6) | collective-permute-done | bytes 65568 | tf_op jit(solution)/shard_map/ppermute | solution.py:268
  61.7 0.7 collective-permute-done.4.n0_ref
  63.1 6.7 %shard_map.81 = f32[64,6,128]{2,1,0:T(8,128)} custom-call(s32[4]{0:T(128)} %add_convert_fusion.edge_ref, f32[128,128]{1,0:T(8,128)} %get-tuple-element.21.forward_ref, f32[256,128]{1,0:T(8,128)} %get-tuple-element.22.given_ref, f32[128,128]{1,0:T(8,128)} %copy-done.11, f32[128,128]{1,0:T(8,128)} %copy-done.10, f32[128,128]{1,0:T(8,128)} %copy-done.8, ...), custom_call_target="tpu_custom_call" | custom-call | flops 4000000000 | bytes 500000 | tf_op jit(solution)/shard_map/pallas_call | solution.py:326
  69.8 19.1 %all_to_all.10.in_ref = f32[64,6,128]{2,1,0:T(8,128)} all-to-all(f32[64,6,128]{2,1,0:T(8,128)} %shard_map.81), channel_id=1, replica_groups=mesh['ah'=2,'am'=2,'al'=2,'b'=4,'c'=2,'gx'=2,'gy'=2] {'ah','am','al','b'..., dimensions={0} | all-to-all | bytes 393216 | tf_op jit(solution)/shard_map/all_to_all | solution.py:333
  88.9 1.7 %shard_map.82 = (f32[2,16,512]{2,1,0:T(8,128)}, f32[2,16,512]{2,1,0:T(8,128)}) custom-call(s32[2]{0:T(128)} %pad_add_fusion.where_ref, f32[64,6,128]{2,1,0:T(8,128)} %all_to_all.10.in_ref), custom_call_target="tpu_custom_call" | custom-call | flops 1000000 | bytes 500000 | tf_op jit(solution)/shard_map/pallas_call | solution.py:334
  90.6 1.5 %reshape.22 = f32[2,4,4,512]{3,2,1,0:T(4,128)} reshape(f32[2,16,512]{2,1,0:T(8,128)} %get-tuple-element.24) | data formatting | bytes 131072 | tf_op jit(solution)/shard_map/reshape | solution.py:335
  92.1 0.6 reshape.23
  (32 shorter events, 4.5 us)
Async XLA Ops:
  0.6 0.7 copy-start.3
  1.9 1.5 %copy-start.1 = (f32[2,4,4,512]{3,2,1,0:T(4,128)S(1)}, f32[2,4,4,512]{3,2,1,0:T(4,128)}, u32[]{:S(2)}) copy-start(f32[2,4,4,512]{3,2,1,0:T(4,128)} %param.7) | copy-start | bytes 196612
  6.5 28.1 %all-to-all-start = ((f32[64,6,128]{2,1,0:T(8,128)}), f32[64,6,128]{2,1,0:T(8,128)S(1)}, u32[]{:S(2)}, u32[]{:S(2)}) async-start(f32[64,6,128]{2,1,0:T(8,128)} %shard_map.77), calls=%async_computation | async-start | bytes 524288 | tf_op jit(solution)/shard_map/all_to_all | solution.py:292
  34.5 0.7 copy-start
  37.0 10.9 %collective-permute-start.3 = (f32[128,128]{1,0:T(8,128)}, f32[128,128]{1,0:T(8,128)S(1)}, u32[]{:S(2)}, u32[]{:S(2)}) collective-permute-start(f32[128,128]{1,0:T(8,128)} %get-tuple-element.15.start_ref), channel_id=1, source_target_pairs={{0,2},{8,0},{16,8},{24,16},{26,24},{18,26},{10,18},{2,10},{1,3},{9... | collective-permute-start | bytes 196616 | tf_op jit(solution)/shard_map/ppermute | solution.py:268
  38.5 9.4 %collective-permute-start.2 = (f32[128,128]{1,0:T(8,128)}, f32[128,128]{1,0:T(8,128)S(1)}, u32[]{:S(2)}, u32[]{:S(2)}) collective-permute-start(f32[128,128]{1,0:T(8,128)} %get-tuple-element.15.start_ref), channel_id=1, source_target_pairs={{0,8},{8,16},{16,24},{24,26},{26,18},{18,10},{10,2},{2,0},{1,9},{9... | collective-permute-start | bytes 196616 | tf_op jit(solution)/shard_map/ppermute | solution.py:268
  39.0 8.9 %collective-permute-start.1 = (f32[128,128]{1,0:T(8,128)}, f32[128,128]{1,0:T(8,128)S(1)}, u32[]{:S(2)}, u32[]{:S(2)}) collective-permute-start(f32[128,128]{1,0:T(8,128)} %get-tuple-element.15.start_ref), channel_id=1, source_target_pairs={{0,1},{32,0},{64,32},{96,64},{97,96},{65,97},{33,65},{1,33},{2,3},... | collective-permute-start | bytes 196616 | tf_op jit(solution)/shard_map/ppermute | solution.py:268
  39.7 8.2 %collective-permute-start = (f32[128,128]{1,0:T(8,128)}, f32[128,128]{1,0:T(8,128)S(1)}, u32[]{:S(2)}, u32[]{:S(2)}) collective-permute-start(f32[128,128]{1,0:T(8,128)} %get-tuple-element.15.start_ref), channel_id=1, source_target_pairs={{0,32},{32,64},{64,96},{96,97},{97,65},{65,33},{33,1},{1,0},{2,34}... | collective-permute-start | bytes 196616 | tf_op jit(solution)/shard_map/ppermute | solution.py:268
  47.8 0.6 copy-start.4
  47.9 0.7 copy-start.5
  47.9 0.7 copy-start.7
  47.9 0.6 copy-start.9
  55.2 4.5 %collective-permute-start.7 = (f32[128,128]{1,0:T(8,128)}, f32[128,128]{1,0:T(8,128)S(1)}, u32[]{:S(2)}, u32[]{:S(2)}) collective-permute-start(f32[128,128]{1,0:T(8,128)} %get-tuple-element.21.forward_ref), channel_id=1, source_target_pairs={{0,2},{8,0},{16,8},{24,16},{26,24},{18,26},{10,18},{2,10},{1,3},{9... | collective-permute-start | bytes 196616 | tf_op jit(solution)/shard_map/ppermute | solution.py:268
  56.8 4.5 %collective-permute-start.6 = (f32[128,128]{1,0:T(8,128)}, f32[128,128]{1,0:T(8,128)S(1)}, u32[]{:S(2)}, u32[]{:S(2)}) collective-permute-start(f32[128,128]{1,0:T(8,128)} %get-tuple-element.21.forward_ref), channel_id=1, source_target_pairs={{0,8},{8,16},{16,24},{24,26},{26,18},{18,10},{10,2},{2,0},{1,9},{9... | collective-permute-start | bytes 196616 | tf_op jit(solution)/shard_map/ppermute | solution.py:268
  57.3 4.5 %collective-permute-start.5 = (f32[128,128]{1,0:T(8,128)}, f32[128,128]{1,0:T(8,128)S(1)}, u32[]{:S(2)}, u32[]{:S(2)}) collective-permute-start(f32[128,128]{1,0:T(8,128)} %get-tuple-element.21.forward_ref), channel_id=1, source_target_pairs={{0,1},{32,0},{64,32},{96,64},{97,96},{65,97},{33,65},{1,33},{2,3},... | collective-permute-start | bytes 196616 | tf_op jit(solution)/shard_map/ppermute | solution.py:268
  57.9 4.5 %collective-permute-start.4 = (f32[128,128]{1,0:T(8,128)}, f32[128,128]{1,0:T(8,128)S(1)}, u32[]{:S(2)}, u32[]{:S(2)}) collective-permute-start(f32[128,128]{1,0:T(8,128)} %get-tuple-element.21.forward_ref), channel_id=1, source_target_pairs={{0,32},{32,64},{64,96},{96,97},{97,65},{65,33},{33,1},{1,0},{2,34}... | collective-permute-start | bytes 196616 | tf_op jit(solution)/shard_map/ppermute | solution.py:268
  59.7 2.7 %copy-start.6 = (f32[128,128]{1,0:T(8,128)}, f32[128,128]{1,0:T(8,128)S(1)}, u32[]{:S(2)}) copy-start(f32[128,128]{1,0:T(8,128)S(1)} %collective-permute-done.7.n3_ref) | copy-start | bytes 196612
  61.2 1.2 %copy-start.8 = (f32[128,128]{1,0:T(8,128)}, f32[128,128]{1,0:T(8,128)S(1)}, u32[]{:S(2)}) copy-start(f32[128,128]{1,0:T(8,128)S(1)} %collective-permute-done.6.n2_ref) | copy-start | bytes 196612
  61.7 0.7 copy-start.10
  62.4 0.6 copy-start.11
  90.6 1.5 %copy-start.2 = (f32[2,16,512]{2,1,0:T(8,128)S(1)}, f32[2,16,512]{2,1,0:T(8,128)}, u32[]{:S(2)}) copy-start(f32[2,16,512]{2,1,0:T(8,128)} %get-tuple-element.25) | copy-start | bytes 196612
where the time goes:
time: 93.3 us; the launch traced here: 92.8 us
  Pallas kernels  25.4 us (27%)
  starting transfers between devices  22.7 us (24%)
  blocking collectives  19.1 us (20%)
  waiting for transfers between devices  15.9 us (17%)
  local copies, waits for them, and re-layouts  7.62 us (8%)
  other arithmetic  1.25 us (1%)
    all_to_all x1, blocking collectives, per_device(): returned = lax.all_to_all(ready, GZ, 0, 0, tiled=True)  19.1 us
    all_to_all x1, starting transfers between devices, per_device(): arrived = lax.all_to_all(packed, GZ, 0, 0, tiled=True)  14.6 us
    all_to_all x1, waiting for transfers between devices, per_device(): arrived = lax.all_to_all(packed, GZ, 0, 0, tiled=True)  12.8 us
    ppermute x8, starting transfers between devices, moved(): return lax.ppermute(value, axes, pairs)  8.1 us
    pallas_call x1, Pallas kernels, per_device(): call(tables_kernel, (shape(7, 256, 256, dtype=BF16), mask, mask, maps, ma...  6.81 us
    pallas_call x1, Pallas kernels, per_device(): call(backward_kernel, shape(PEERS, SLOTS, LANES), [SMEM] + [VMEM] * 10, c...  6.73 us
    pallas_call x1, Pallas kernels, per_device(): call(forward_kernel, (shape(ROWS, LANES), shape(2 * ROWS, LANES)), [SMEM]...  6.69 us
    ppermute x8, waiting for transfers between devices, moved(): return lax.ppermute(value, axes, pairs)  3.13 us
  transfers between devices with their start and end apart: 9, of which 5 were waited for; matrix products, arithmetic and copies ran while one was open for 1% of the time, Pallas kernels for 7%

commit v1 on v0

--- a/solution.py
+++ b/solution.py
@@ -57,37 +57,46 @@
     return (y ^ flip_y) * 8 + (x ^ flip_x) * 2
 
 
-def pack_kernel(where_ref, mat_ref, rhs_ref, start_ref, out_ref):
-    flip_x, flip_y = where_ref[0], where_ref[1]
+def flips():
+    return lax.axis_index("gx") * 3, lax.axis_index("gy") * 3
+
+
+def pack_kernel(mat_ref, rhs_ref, start_ref, out_ref):
+    flip_x, flip_y = flips()
     for y in range(4):
         for x in range(4):
             block = block_of(y, x, flip_y, flip_x)
-            cell = y * 4 + x
             for p in range(2):
-                kind = jnp.full((1, LANES), mat_ref[p, cell].astype(F32))
+                kind = jnp.full((1, LANES), mat_ref[p, y, x].astype(F32))
                 for part in range(4):
                     lanes = slice(part * LANES, (part + 1) * LANES)
                     slot = block + (part // 2) * 32 + part % 2
-                    out_ref[slot, p : p + 1, :] = rhs_ref[p, cell : cell + 1, lanes]
-                    out_ref[slot, 2 + p : 3 + p, :] = start_ref[p, cell : cell + 1, lanes]
+                    out_ref[slot, p : p + 1, :] = rhs_ref[p, y, x : x + 1, lanes]
+                    out_ref[slot, 2 + p : 3 + p, :] = start_ref[p, y, x : x + 1, lanes]
                     out_ref[slot, 4 + p : 5 + p, :] = kind
 
 
-def unpack_kernel(where_ref, in_ref, forward_ref, backward_ref):
-    flip_x, flip_y = where_ref[0], where_ref[1]
+def unpack_kernel(in_ref, forward_ref, backward_ref):
+    flip_x, flip_y = flips()
     for y in range(4):
         for x in range(4):
             block = block_of(y, x, flip_y, flip_x)
-            cell = y * 4 + x
             for part in range(4):
                 lanes = slice(part * LANES, (part + 1) * LANES)
                 slot = block + (part // 2) * 32 + part % 2
                 for p in range(2):
-                    forward_ref[p, cell : cell + 1, lanes] = in_ref[slot, p : p + 1, :]
-                    backward_ref[p, cell : cell + 1, lanes] = in_ref[slot, 2 + p : 3 + p, :]
-
-
-def arrange_kernel(in_ref, rhs_ref, start_ref, kind_ref):
+                    forward_ref[p, y, x : x + 1, lanes] = in_ref[slot, p : p + 1, :]
+                    backward_ref[p, y, x : x + 1, lanes] = in_ref[slot, 2 + p : 3 + p, :]
+
+
+def masks_of(kind):
+    half = (lax.broadcasted_iota(jnp.int32, kind.shape, 1) >= DOFS).astype(F32)
+    mask_a = jnp.where(kind == half, 1.0, 0.0).astype(BF16)
+    mask_b = jnp.where(kind == half + 2.0, 1.0, 0.0).astype(BF16)
+    return mask_a, mask_b
+
+
+def arrange_kernel(in_ref, rhs_ref, start_ref, kind_ref, mask_a_ref, mask_b_ref):
     for step in range(STEPS):
         for chunk in range(CHUNKS):
             block, p = chunk * 4 + step // 2, step % 2
@@ -95,17 +104,12 @@
             rhs_ref[row : row + 1, :] = in_ref[block, p : p + 1, :]
             start_ref[row : row + 1, :] = in_ref[block, 2 + p : 3 + p, :]
             kind_ref[row : row + 1, :] = in_ref[block, 4 + p : 5 + p, :]
-
-
-def masks_of(kind):
-    half = (lax.broadcasted_iota(jnp.int32, kind.shape, 1) >= DOFS).astype(F32)
-    mask_a = jnp.where(kind == half, 1.0, 0.0).astype(BF16)
-    mask_b = jnp.where(kind == half + 2.0, 1.0, 0.0).astype(BF16)
-    return mask_a, mask_b
-
-
-def tables_kernel(diag_ref, z_ref, side_ref, kind_ref, tables_ref, mask_a_ref, mask_b_ref, map_f_ref, map_b_ref,
-                  plain_ref, run_ref, wide_ref):
+    mask_a, mask_b = masks_of(kind_ref[...])
+    mask_a_ref[...] = mask_a
+    mask_b_ref[...] = mask_b
+
+
+def tables_kernel(diag_ref, z_ref, side_ref, tables_ref, plain_ref):
     for m in range(KINDS):
         inverse = jnp.concatenate([diag_ref[m], diag_ref[m]], axis=1)
         left = jnp.concatenate([z_ref[m].reshape(2 * DOFS, DOFS), side_ref[m].reshape(4 * DOFS, DOFS)], axis=0)
@@ -118,33 +122,32 @@
             tables_ref[q, m * DOFS : (m + 1) * DOFS, LANES:] = low[rows]
         for q in range(2):
             plain_ref[q, m] = joined[q * DOFS : (q + 1) * DOFS]
-    mask_a, mask_b = masks_of(kind_ref[...])
-    mask_a_ref[...] = mask_a
-    mask_b_ref[...] = mask_b
-
-    for q, map_ref in ((0, map_f_ref), (1, map_b_ref)):
-        order = list(range(STEPS)) if q == 0 else list(reversed(range(STEPS)))
-        for chunk in range(CHUNKS):
-            row = order[0] * CHUNKS + chunk
-            kind = jnp.broadcast_to(kind_ref[row : row + 1, :], (DOFS, LANES))
-            first = jnp.where(kind == 0.0, plain_ref[q, 0], plain_ref[q, 1])
-            second = jnp.where(kind == 2.0, plain_ref[q, 2], plain_ref[q, 3])
-            run_ref[chunk] = jnp.where(kind < 2.0, first, second)
-        for step in order[1:]:
-            for group in range(4):
-                for k in range(4):
-                    chunk = group * 4 + k
-                    row = step * CHUNKS + chunk
-                    a = jnp.broadcast_to(mask_a[row : row + 1, :], (DOFS, LANES))
-                    b = jnp.broadcast_to(mask_b[row : row + 1, :], (DOFS, LANES))
-                    wide_ref[k * 2 * DOFS : (k + 1) * 2 * DOFS, :] = widened(run_ref[chunk], a, b)
-                product = jnp.dot(wide_ref[...], tables_ref[q], preferred_element_type=F32)
-                for k in range(4):
-                    run_ref[group * 4 + k] = fold(product[k * 2 * DOFS : (k + 1) * 2 * DOFS])
-        for chunk in range(CHUNKS):
-            high, low = split(run_ref[chunk])
-            map_ref[chunk, :DOFS, :] = high
-            map_ref[chunk, DOFS:, :] = low
+
+
+def maps_kernel(q, kind_ref, mask_a_ref, mask_b_ref, tables_ref, plain_ref, after_ref, map_ref, run_ref, wide_ref):
+    order = list(range(STEPS)) if q == 0 else list(reversed(range(STEPS)))
+    for chunk in range(CHUNKS):
+        row = order[0] * CHUNKS + chunk
+        kind = jnp.broadcast_to(kind_ref[row : row + 1, :], (DOFS, LANES))
+        first = jnp.where(kind == 0.0, plain_ref[q, 0], plain_ref[q, 1])
+        second = jnp.where(kind == 2.0, plain_ref[q, 2], plain_ref[q, 3])
+        run_ref[chunk] = jnp.where(kind < 2.0, first, second)
+    for step in order[1:]:
+        rows = pl.ds(step * CHUNKS, CHUNKS)
+        mask_a, mask_b = mask_a_ref[rows, :], mask_b_ref[rows, :]
+        for group in range(4):
+            for k in range(4):
+                chunk = group * 4 + k
+                a = jnp.broadcast_to(mask_a[chunk : chunk + 1, :], (DOFS, LANES))
+                b = jnp.broadcast_to(mask_b[chunk : chunk + 1, :], (DOFS, LANES))
+                wide_ref[k * 2 * DOFS : (k + 1) * 2 * DOFS, :] = widened(run_ref[chunk], a, b)
+            product = jnp.dot(wide_ref[...], tables_ref[q], preferred_element_type=F32)
+            for k in range(4):
+                run_ref[group * 4 + k] = fold(product[k * 2 * DOFS : (k + 1) * 2 * DOFS])
+    for chunk in range(CHUNKS):
+        high, low = split(run_ref[chunk])
+        map_ref[chunk, :DOFS, :] = high
+        map_ref[chunk, DOFS:, :] = low
 
 
 def chain(const_ref, mask_a_ref, mask_b_ref, table_ref, map_ref, ends_ref, heads_ref, out_ref, descending):
@@ -195,6 +198,14 @@
         out_ref[pl.ds(step * CHUNKS, CHUNKS), :] = jnp.where(low, state[:CHUNKS], state[CHUNKS:])
 
 
+def beside_inside(refs):
+    x, y = lax.axis_index("b"), lax.axis_index("am") * 2 + lax.axis_index("al")
+    x = jnp.where(lax.axis_index("gx") == 1, 7 - x, x)
+    y = jnp.where(lax.axis_index("gy") == 1, 7 - y, y)
+    inside = (y > 0, y < 7, x > 0, x < 7)
+    return [jnp.where(here, ref[...], 0.0) for here, ref in zip(inside, refs)]
+
+
 def neighbour_terms(wide_ref, pieces, mask_a, mask_b, tables_ref, first):
     for k, piece in enumerate(pieces):
         wide_ref[:, k * 256 : (k + 1) * 256] = widened(doubled(piece), mask_a, mask_b)
@@ -209,15 +220,13 @@
     return jnp.concatenate([mask, mask], axis=0)
 
 
-def forward_kernel(edge_ref, rhs_ref, start_ref, n0_ref, n1_ref, n2_ref, n3_ref, mask_a_ref, mask_b_ref, tables_ref,
+def forward_kernel(rhs_ref, start_ref, n0_ref, n1_ref, n2_ref, n3_ref, mask_a_ref, mask_b_ref, tables_ref,
                    map_ref, forward_ref, given_ref, const_ref, ends_ref, heads_ref, wide_ref):
     mask_a, mask_b = both(mask_a_ref[...]), both(mask_b_ref[...])
     start = start_ref[...]
     following = jnp.concatenate([start[1:CHUNKS], jnp.zeros((1, LANES), F32)], axis=0)
     upper = jnp.concatenate([start[CHUNKS:], following], axis=0)
-    pieces = [upper]
-    for k, ref in enumerate((n0_ref, n1_ref, n2_ref, n3_ref)):
-        pieces.append(jnp.where(edge_ref[k] > 0, ref[...], 0.0))
+    pieces = [upper] + beside_inside((n0_ref, n1_ref, n2_ref, n3_ref))
     given = neighbour_terms(wide_ref, pieces, mask_a, mask_b, tables_ref, 1)
     given_ref[...] = given
     own = widened(doubled(rhs_ref[...]), mask_a, mask_b)
@@ -225,12 +234,10 @@
     chain(const_ref, mask_a_ref, mask_b_ref, tables_ref.at[0], map_ref, ends_ref, heads_ref, forward_ref, False)
 
 
-def backward_kernel(edge_ref, forward_ref, given_ref, n0_ref, n1_ref, n2_ref, n3_ref, mask_a_ref, mask_b_ref,
+def backward_kernel(forward_ref, given_ref, n0_ref, n1_ref, n2_ref, n3_ref, mask_a_ref, mask_b_ref,
                     tables_ref, map_ref, out_ref, const_ref, ends_ref, heads_ref, wide_ref, backward_ref):
     mask_a, mask_b = both(mask_a_ref[...]), both(mask_b_ref[...])
-    pieces = []
-    for k, ref in enumerate((n0_ref, n1_ref, n2_ref, n3_ref)):
-        pieces.append(jnp.where(edge_ref[k] > 0, ref[...], 0.0))
+    pieces = beside_inside((n0_ref, n1_ref, n2_ref, n3_ref))
     terms = neighbour_terms(wide_ref, pieces, mask_a, mask_b, tables_ref, 2)
     const_ref[...] = doubled(forward_ref[...]) + (given_ref[...] - terms)
     chain(const_ref, mask_a_ref, mask_b_ref, tables_ref.at[1], map_ref, ends_ref, heads_ref, backward_ref, True)
@@ -256,6 +263,7 @@
         out_specs=jax.tree.map(lambda _: VMEM, outs),
         scratch_shapes=scratch,
         cost_estimate=pl.CostEstimate(flops=flops, bytes_accessed=500000, transcendentals=0),
+        compiler_params=pltpu.CompilerParams(vmem_limit_bytes=16 * 1024 * 1024),
     )
 
 
@@ -278,37 +286,29 @@
 
 
 def per_device(rhs_field, start_field, material, diag_inverse, z_blocks, side_blocks):
-    gx, gy = lax.axis_index("gx"), lax.axis_index("gy")
-    where = jnp.stack([gx * 3, gy * 3]).astype(jnp.int32)
-    x = lax.axis_index("b")
-    y = lax.axis_index("am") * 2 + lax.axis_index("al")
-    x = jnp.where(gx == 1, 7 - x, x)
-    y = jnp.where(gy == 1, 7 - y, y)
-    edge = jnp.stack([y > 0, y < 7, x > 0, x < 7]).astype(jnp.int32)
-
-    packed = call(pack_kernel, shape(PEERS, SLOTS, LANES), [SMEM, SMEM, VMEM, VMEM])(
-        where, material.reshape(2, 16), rhs_field.reshape(2, 16, 512), start_field.reshape(2, 16, 512)
-    )
+    mask = shape(ROWS, LANES, dtype=BF16)
+    field = shape(ROWS, LANES)
+    packed = call(pack_kernel, shape(PEERS, SLOTS, LANES), [SMEM, VMEM, VMEM])(material, rhs_field, start_field)
     arrived = lax.all_to_all(packed, GZ, 0, 0, tiled=True)
-    rhs, start, kind = call(
-        arrange_kernel, (shape(ROWS, LANES), shape(ROWS, LANES), shape(ROWS, LANES)), [VMEM]
-    )(arrived)
+    tables, plain = call(
+        tables_kernel,
+        (shape(7, 256, 256, dtype=BF16), shape(2, KINDS, DOFS, LANES)),
+        [VMEM] * 3,
+        flops=4000000000,
+    )(diag_inverse, z_blocks, side_blocks)
+    rhs, start, kind, mask_a, mask_b = call(arrange_kernel, (field, field, field, mask, mask), [VMEM])(arrived)
     beside = neighbours(start)
 
-    maps = shape(CHUNKS, 2 * DOFS, LANES, dtype=BF16)
-    mask = shape(ROWS, LANES, dtype=BF16)
-    tables, mask_a, mask_b, map_f, map_b = call(
-        tables_kernel,
-        (shape(7, 256, 256, dtype=BF16), mask, mask, maps, maps),
-        [VMEM] * 4,
-        [
-            pltpu.VMEM((2, KINDS, DOFS, LANES), F32),
-            pltpu.VMEM((CHUNKS, DOFS, LANES), F32),
-            pltpu.VMEM((8 * DOFS, 256), BF16),
-        ],
-        flops=4000000000,
-    )(diag_inverse, z_blocks, side_blocks, kind)
-
+    def maps(q, after):
+        return call(
+            functools.partial(maps_kernel, q),
+            shape(CHUNKS, 2 * DOFS, LANES, dtype=BF16),
+            [VMEM] * 5 + [pl.BlockSpec(memory_space=pl.ANY)],
+            [pltpu.VMEM((CHUNKS, DOFS, LANES), F32), pltpu.VMEM((8 * DOFS, 256), BF16)],
+            flops=4000000000,
+        )(kind, mask_a, mask_b, tables, plain, after)
+
+    map_f = maps(0, start)
     chain_scratch = [
         pltpu.VMEM((2 * ROWS, LANES), F32),
         pltpu.VMEM((2 * CHUNKS, LANES), F32),
@@ -316,23 +316,24 @@
     ]
     forward, given = call(
         forward_kernel,
-        (shape(ROWS, LANES), shape(2 * ROWS, LANES)),
-        [SMEM] + [VMEM] * 10,
+        (field, shape(2 * ROWS, LANES)),
+        [VMEM] * 10,
         chain_scratch + [pltpu.VMEM((4 * ROWS, 5 * 256), BF16)],
         flops=4000000000,
-    )(edge, rhs, start, *beside, mask_a, mask_b, tables, map_f)
+    )(rhs, start, *beside, mask_a, mask_b, tables, map_f)
 
     beside = neighbours(forward)
+    map_b = maps(1, forward)
     ready = call(
         backward_kernel,
         shape(PEERS, SLOTS, LANES),
-        [SMEM] + [VMEM] * 10,
+        [VMEM] * 10,
         chain_scratch + [pltpu.VMEM((4 * ROWS, 4 * 256), BF16), pltpu.VMEM((ROWS, LANES), F32)],
         flops=4000000000,
-    )(edge, forward, given, *beside, mask_a, mask_b, tables, map_b)
+    )(forward, given, *beside, mask_a, mask_b, tables, map_b)
     returned = lax.all_to_all(ready, GZ, 0, 0, tiled=True)
-    out_f, out_b = call(unpack_kernel, (shape(2, 16, 512), shape(2, 16, 512)), [SMEM, VMEM])(where, returned)
-    return out_f.reshape(rhs_field.shape), out_b.reshape(rhs_field.shape)
+    cells = shape(*rhs_field.shape)
+    return call(unpack_kernel, (cells, cells), [VMEM])(returned)
 
 
 def solution(mesh):

time: 93.3 us -> 76.3 us (0.82)
  Pallas kernels: 25.4 us -> 16.3 us
  local copies, waits for them, and re-layouts: 7.62 us -> 2.37 us
  other arithmetic: 1.25 us -> 0 us
  waiting for transfers between devices: 15.9 us -> 14.8 us
    pallas_call x6 -> x8, Pallas kernels: 25.4 us -> 16.3 us  [the longest x1 4.49 us: per_device(): call(forward_kernel, (field, shape(2 * ROWS, LANES)), [VMEM] * 10, chain_...]
    reshape x5 -> x0, local copies, waits for them, and re-layouts: 4.96 us -> none  [the longest x2 2.17 us: per_device(): return (out_f.reshape(rhs_field.shape), out_b.reshape(rhs_field.shape))]
    unnamed x24 -> x12, local copies, waits for them, and re-layouts: 2.66 us -> 2.37 us
  transfers between devices with their start and end apart: 9 -> 9, of which waited for: 5 -> 5; matrix products, arithmetic and copies ran while one was open for 1% -> 0% of each run, Pallas kernels for 7% -> 7%
where the time goes in v1:
time: 76.3 us; the launch traced here: 76 us
  starting transfers between devices  22.9 us (30%)
  blocking collectives  18.9 us (25%)
  Pallas kernels  16.3 us (21%)
  waiting for transfers between devices  14.8 us (19%)
  local copies, waits for them, and re-layouts  2.37 us (3%)
    all_to_all x1, blocking collectives, per_device(): returned = lax.all_to_all(ready, GZ, 0, 0, tiled=True)  18.9 us
    all_to_all x1, starting transfers between devices, per_device(): arrived = lax.all_to_all(packed, GZ, 0, 0, tiled=True)  14.8 us
    all_to_all x1, waiting for transfers between devices, per_device(): arrived = lax.all_to_all(packed, GZ, 0, 0, tiled=True)  12.5 us
    ppermute x8, starting transfers between devices, moved(): return lax.ppermute(value, axes, pairs)  8.13 us
    pallas_call x1, Pallas kernels, per_device(): call(forward_kernel, (field, shape(2 * ROWS, LANES)), [VMEM] * 10, chain_...  4.49 us
    pallas_call x1, Pallas kernels, per_device(): call(backward_kernel, shape(PEERS, SLOTS, LANES), [VMEM] * 10, chain_scra...  4.42 us
    pallas_call x2, Pallas kernels, maps(): call(functools.partial(maps_kernel, q), shape(CHUNKS, 2 * DOFS, LANES, dt...  4.17 us
    unnamed x12, local copies, waits for them, and re-layouts  2.37 us
  transfers between devices with their start and end apart: 9, of which 5 were waited for; matrix products, arithmetic and copies ran while one was open for 0% of the time, Pallas kernels for 7%

profile of v1, /device:TPU:2, one launch (start us, length us, event | category | flops | bytes accessed | tf_op | source)
XLA Modules:
  0.0 76.0 jit_solution(16107529867595469381)
XLA Ops:
  0.6 0.8 %copy-done = f32[2,4,4,512]{3,2,1,0:T(4,128)S(1)} copy-done((f32[2,4,4,512]{3,2,1,0:T(4,128)S(1)}, f32[2,4,4,512]{3,2,1,0:T(4,128)}, u32[]{:S(2)}) %copy-start) | copy-done | bytes 65560
  1.5 0.8 %copy-done.1 = f32[2,4,4,512]{3,2,1,0:T(4,128)S(1)} copy-done((f32[2,4,4,512]{3,2,1,0:T(4,128)S(1)}, f32[2,4,4,512]{3,2,1,0:T(4,128)}, u32[]{:S(2)}) %copy-start.1) | copy-done | bytes 65560
  2.3 0.7 copy-done.2
  3.0 1.4 %shard_map.77 = f32[64,6,128]{2,1,0:T(8,128)} custom-call(s32[2,4,4]{2,1,0:T(4,128)S(1)} %copy-done.2, f32[2,4,4,512]{3,2,1,0:T(4,128)S(1)} %copy-done, f32[2,4,4,512]{3,2,1,0:T(4,128)S(1)} %copy-done.1), custom_call_target="tpu_custom_call" | custom-call | flops 1000000 | bytes 500000 | tf_op jit(solution)/shard_map/pallas_call | solution.py:291
  4.4 14.8 %all-to-all-start = ((f32[64,6,128]{2,1,0:T(8,128)}), f32[64,6,128]{2,1,0:T(8,128)S(1)}, u32[]{:S(2)}, u32[]{:S(2)}) async-start(f32[64,6,128]{2,1,0:T(8,128)} %shard_map.77), calls=%async_computation | async-start | bytes 524288 | tf_op jit(solution)/shard_map/all_to_all | solution.py:292
  19.3 0.9 %shard_map.79 = (bf16[7,256,256]{2,1,0:T(8,128)(2,1)S(1)}, f32[2,4,64,128]{3,2,1,0:T(8,128)S(1)}) custom-call(f32[4,64,64]{2,1,0:T(8,128)S(1)} %copy-done.5, f32[4,2,64,64]{3,2,1,0:T(8,128)S(1)} %copy-done.4, f32[4,4,64,64]{3,2,1,0:T(8,128)S(1)} %copy-done.3), custom_call_target="tpu_custom_call" | custom-call | flops 4000000000 | bytes 500000 | tf_op jit(solution)/shard_map/pallas_call | solution.py:293
  20.1 12.5 %all-to-all-done.in_ref = f32[64,6,128]{2,1,0:T(8,128)S(1)} async-done(((f32[64,6,128]{2,1,0:T(8,128)}), f32[64,6,128]{2,1,0:T(8,128)S(1)}, u32[]{:S(2)}, u32[]{:S(2)}) %all-to-all-start) | async-done | bytes 196640 | tf_op jit(solution)/shard_map/all_to_all | solution.py:292
  32.6 0.2 shard_map.78
  32.8 1.5 %collective-permute-start.3 = (f32[128,128]{1,0:T(8,128)S(1)}, f32[128,128]{1,0:T(8,128)S(1)}, u32[]{:S(2)}, u32[]{:S(2)}) collective-permute-start(f32[128,128]{1,0:T(8,128)S(1)} %get-tuple-element.12.after_ref.start_ref), channel_id=1, source_target_pairs={{0,2},{8,0},{16,8},{24,16},{26,24},{18,26},{10,18},{2,10},{1,3},{9... | collective-permute-start | bytes 196616 | tf_op jit(solution)/shard_map/ppermute | solution.py:276
  34.3 0.5 collective-permute-start.2
  34.8 0.7 collective-permute-start.1
  35.5 1.3 %collective-permute-start = (f32[128,128]{1,0:T(8,128)S(1)}, f32[128,128]{1,0:T(8,128)S(1)}, u32[]{:S(2)}, u32[]{:S(2)}) collective-permute-start(f32[128,128]{1,0:T(8,128)S(1)} %get-tuple-element.12.after_ref.start_ref), channel_id=1, source_target_pairs={{0,32},{32,64},{64,96},{96,97},{97,65},{65,33},{33,1},{1,0},{2,34}... | collective-permute-start | bytes 196616 | tf_op jit(solution)/shard_map/ppermute | solution.py:276
  36.8 2.1 %shard_map.80.map_ref = bf16[16,128,128]{2,1,0:T(8,128)(2,1)S(1)} custom-call(f32[128,128]{1,0:T(8,128)S(1)} %get-tuple-element.16.kind_ref, bf16[128,128]{1,0:T(8,128)(2,1)S(1)} %get-tuple-element.13.mask_a_ref, bf16[128,128]{1,0:T(8,128)(2,1)S(1)} %get-tuple-element.14.mask_b_ref, bf16[7,256,256]{2,1,0:T(8,128)(2,1)S(1)} %get-tuple-element.15.tables_ref, ...), custom_call_target="tpu_custom_call" | custom-call | flops 4000000000 | bytes 500000 | tf_op jit(solution)/shard_map/pallas_call | solution.py:303
  39.1 0.7 collective-permute-done.n0_ref
  39.8 4.5 %shard_map.81 = (f32[128,128]{1,0:T(8,128)S(1)}, f32[256,128]{1,0:T(8,128)S(1)}) custom-call(f32[128,128]{1,0:T(8,128)S(1)} %get-tuple-element.11.rhs_ref, f32[128,128]{1,0:T(8,128)S(1)} %get-tuple-element.12.after_ref.start_ref, f32[128,128]{1,0:T(8,128)S(1)} %collective-permute-done.n0_ref, f32[128,128]{1,0:T(8,128)S(1)} %collective-permute-done.1.n1_ref, ...), custom_call_target="tpu_custom_call" | custom-call | flops 4000000000 | bytes 500000 | tf_op jit(solution)/shard_map/pallas_call | solution.py:317
  44.3 1.5 %collective-permute-start.7 = (f32[128,128]{1,0:T(8,128)S(1)}, f32[128,128]{1,0:T(8,128)S(1)}, u32[]{:S(2)}, u32[]{:S(2)}) collective-permute-start(f32[128,128]{1,0:T(8,128)S(1)} %get-tuple-element.18.after_ref.forward_ref), channel_id=1, source_target_pairs={{0,2},{8,0},{16,8},{24,16},{26,24},{18,26},{10,18},{2,10},{1,3},{9... | collective-permute-start | bytes 196616 | tf_op jit(solution)/shard_map/ppermute | solution.py:276
  45.8 0.5 collective-permute-start.6
  46.3 1.3 %collective-permute-start.5 = (f32[128,128]{1,0:T(8,128)S(1)}, f32[128,128]{1,0:T(8,128)S(1)}, u32[]{:S(2)}, u32[]{:S(2)}) collective-permute-start(f32[128,128]{1,0:T(8,128)S(1)} %get-tuple-element.18.after_ref.forward_ref), channel_id=1, source_target_pairs={{0,1},{32,0},{64,32},{96,64},{97,96},{65,97},{33,65},{1,33},{2,3},... | collective-permute-start | bytes 196616 | tf_op jit(solution)/shard_map/ppermute | solution.py:276
  47.7 0.7 collective-permute-start.4
  48.3 2.1 %shard_map.82.map_ref = bf16[16,128,128]{2,1,0:T(8,128)(2,1)S(1)} custom-call(f32[128,128]{1,0:T(8,128)S(1)} %get-tuple-element.16.kind_ref, bf16[128,128]{1,0:T(8,128)(2,1)S(1)} %get-tuple-element.13.mask_a_ref, bf16[128,128]{1,0:T(8,128)(2,1)S(1)} %get-tuple-element.14.mask_b_ref, bf16[7,256,256]{2,1,0:T(8,128)(2,1)S(1)} %get-tuple-element.15.tables_ref, ...), custom_call_target="tpu_custom_call" | custom-call | flops 4000000000 | bytes 500000 | tf_op jit(solution)/shard_map/pallas_call | solution.py:303
  50.6 1.3 %collective-permute-done.4.n0_ref = f32[128,128]{1,0:T(8,128)S(1)} collective-permute-done((f32[128,128]{1,0:T(8,128)S(1)}, f32[128,128]{1,0:T(8,128)S(1)}, u32[]{:S(2)}, u32[]{:S(2)}) %collective-permute-start.4) | collective-permute-done | bytes 65568 | tf_op jit(solution)/shard_map/ppermute | solution.py:276
  51.9 4.4 %shard_map.83 = f32[64,6,128]{2,1,0:T(8,128)S(1)} custom-call(f32[128,128]{1,0:T(8,128)S(1)} %get-tuple-element.18.after_ref.forward_ref, f32[256,128]{1,0:T(8,128)S(1)} %get-tuple-element.19.given_ref, f32[128,128]{1,0:T(8,128)S(1)} %collective-permute-done.4.n0_ref, f32[128,128]{1,0:T(8,128)S(1)} %collective-permute-done.5.n1_ref, ...), custom_call_target="tpu_custom_call" | custom-call | flops 4000000000 | bytes 500000 | tf_op jit(solution)/shard_map/pallas_call | solution.py:327
  56.4 18.9 %all_to_all.10.in_ref = f32[64,6,128]{2,1,0:T(8,128)S(1)} all-to-all(f32[64,6,128]{2,1,0:T(8,128)S(1)} %shard_map.83), channel_id=1, replica_groups=mesh['ah'=2,'am'=2,'al'=2,'b'=4,'c'=2,'gx'=2,'gy'=2] {'ah','am','al','b'..., dimensions={0} | all-to-all | bytes 393216 | tf_op jit(solution)/shard_map/all_to_all | solution.py:334
  75.2 0.7 shard_map.84
  (15 shorter events, 0.3 us)
Async XLA Ops:
  0.6 0.8 %copy-start = (f32[2,4,4,512]{3,2,1,0:T(4,128)S(1)}, f32[2,4,4,512]{3,2,1,0:T(4,128)}, u32[]{:S(2)}) copy-start(f32[2,4,4,512]{3,2,1,0:T(4,128)} %rhs_ref.1) | copy-start | bytes 196612
  1.5 0.8 %copy-start.1 = (f32[2,4,4,512]{3,2,1,0:T(4,128)S(1)}, f32[2,4,4,512]{3,2,1,0:T(4,128)}, u32[]{:S(2)}) copy-start(f32[2,4,4,512]{3,2,1,0:T(4,128)} %start_ref.1) | copy-start | bytes 196612
  2.3 0.7 copy-start.2
  3.0 16.2 %copy-start.3 = (f32[4,4,64,64]{3,2,1,0:T(8,128)S(1)}, f32[4,4,64,64]{3,2,1,0:T(8,128)}, u32[]{:S(2)}) copy-start(f32[4,4,64,64]{3,2,1,0:T(8,128)} %side_ref.1) | copy-start | bytes 786436
  4.4 14.8 %copy-start.4 = (f32[4,2,64,64]{3,2,1,0:T(8,128)S(1)}, f32[4,2,64,64]{3,2,1,0:T(8,128)}, u32[]{:S(2)}) copy-start(f32[4,2,64,64]{3,2,1,0:T(8,128)} %z_ref.1) | copy-start | bytes 393220
  4.4 14.8 %copy-start.5 = (f32[4,64,64]{2,1,0:T(8,128)S(1)}, f32[4,64,64]{2,1,0:T(8,128)}, u32[]{:S(2)}) copy-start(f32[4,64,64]{2,1,0:T(8,128)} %diag_ref.1) | copy-start | bytes 196612
  4.4 28.2 %all-to-all-start = ((f32[64,6,128]{2,1,0:T(8,128)}), f32[64,6,128]{2,1,0:T(8,128)S(1)}, u32[]{:S(2)}, u32[]{:S(2)}) async-start(f32[64,6,128]{2,1,0:T(8,128)} %shard_map.77), calls=%async_computation | async-start | bytes 524288 | tf_op jit(solution)/shard_map/all_to_all | solution.py:292
  32.8 6.2 %collective-permute-start.3 = (f32[128,128]{1,0:T(8,128)S(1)}, f32[128,128]{1,0:T(8,128)S(1)}, u32[]{:S(2)}, u32[]{:S(2)}) collective-permute-start(f32[128,128]{1,0:T(8,128)S(1)} %get-tuple-element.12.after_ref.start_ref), channel_id=1, source_target_pairs={{0,2},{8,0},{16,8},{24,16},{26,24},{18,26},{10,18},{2,10},{1,3},{9... | collective-permute-start | bytes 196616 | tf_op jit(solution)/shard_map/ppermute | solution.py:276
  34.3 4.6 %collective-permute-start.2 = (f32[128,128]{1,0:T(8,128)S(1)}, f32[128,128]{1,0:T(8,128)S(1)}, u32[]{:S(2)}, u32[]{:S(2)}) collective-permute-start(f32[128,128]{1,0:T(8,128)S(1)} %get-tuple-element.12.after_ref.start_ref), channel_id=1, source_target_pairs={{0,8},{8,16},{16,24},{24,26},{26,18},{18,10},{10,2},{2,0},{1,9},{9... | collective-permute-start | bytes 196616 | tf_op jit(solution)/shard_map/ppermute | solution.py:276
  34.8 4.3 %collective-permute-start.1 = (f32[128,128]{1,0:T(8,128)S(1)}, f32[128,128]{1,0:T(8,128)S(1)}, u32[]{:S(2)}, u32[]{:S(2)}) collective-permute-start(f32[128,128]{1,0:T(8,128)S(1)} %get-tuple-element.12.after_ref.start_ref), channel_id=1, source_target_pairs={{0,1},{32,0},{64,32},{96,64},{97,96},{65,97},{33,65},{1,33},{2,3},... | collective-permute-start | bytes 196616 | tf_op jit(solution)/shard_map/ppermute | solution.py:276
  35.5 4.3 %collective-permute-start = (f32[128,128]{1,0:T(8,128)S(1)}, f32[128,128]{1,0:T(8,128)S(1)}, u32[]{:S(2)}, u32[]{:S(2)}) collective-permute-start(f32[128,128]{1,0:T(8,128)S(1)} %get-tuple-element.12.after_ref.start_ref), channel_id=1, source_target_pairs={{0,32},{32,64},{64,96},{96,97},{97,65},{65,33},{33,1},{1,0},{2,34}... | collective-permute-start | bytes 196616 | tf_op jit(solution)/shard_map/ppermute | solution.py:276
  44.3 6.2 %collective-permute-start.7 = (f32[128,128]{1,0:T(8,128)S(1)}, f32[128,128]{1,0:T(8,128)S(1)}, u32[]{:S(2)}, u32[]{:S(2)}) collective-permute-start(f32[128,128]{1,0:T(8,128)S(1)} %get-tuple-element.18.after_ref.forward_ref), channel_id=1, source_target_pairs={{0,2},{8,0},{16,8},{24,16},{26,24},{18,26},{10,18},{2,10},{1,3},{9... | collective-permute-start | bytes 196616 | tf_op jit(solution)/shard_map/ppermute | solution.py:276
  45.8 4.6 %collective-permute-start.6 = (f32[128,128]{1,0:T(8,128)S(1)}, f32[128,128]{1,0:T(8,128)S(1)}, u32[]{:S(2)}, u32[]{:S(2)}) collective-permute-start(f32[128,128]{1,0:T(8,128)S(1)} %get-tuple-element.18.after_ref.forward_ref), channel_id=1, source_target_pairs={{0,8},{8,16},{16,24},{24,26},{26,18},{18,10},{10,2},{2,0},{1,9},{9... | collective-permute-start | bytes 196616 | tf_op jit(solution)/shard_map/ppermute | solution.py:276
  46.3 4.3 %collective-permute-start.5 = (f32[128,128]{1,0:T(8,128)S(1)}, f32[128,128]{1,0:T(8,128)S(1)}, u32[]{:S(2)}, u32[]{:S(2)}) collective-permute-start(f32[128,128]{1,0:T(8,128)S(1)} %get-tuple-element.18.after_ref.forward_ref), channel_id=1, source_target_pairs={{0,1},{32,0},{64,32},{96,64},{97,96},{65,97},{33,65},{1,33},{2,3},... | collective-permute-start | bytes 196616 | tf_op jit(solution)/shard_map/ppermute | solution.py:276
  47.7 4.3 %collective-permute-start.4 = (f32[128,128]{1,0:T(8,128)S(1)}, f32[128,128]{1,0:T(8,128)S(1)}, u32[]{:S(2)}, u32[]{:S(2)}) collective-permute-start(f32[128,128]{1,0:T(8,128)S(1)} %get-tuple-element.18.after_ref.forward_ref), channel_id=1, source_target_pairs={{0,32},{32,64},{64,96},{96,97},{97,65},{65,33},{33,1},{1,0},{2,34}... | collective-permute-start | bytes 196616 | tf_op jit(solution)/shard_map/ppermute | solution.py:276

commit v2 on v1

--- a/solution.py
+++ b/solution.py
@@ -16,13 +16,13 @@
 LANES = 128
 DOFS = 64
 KINDS = 4
-STEPS = 8
-CHUNKS = 16
+STEPS = 4
+CHUNKS = 128 // STEPS
 ROWS = STEPS * CHUNKS
 PEERS = 64
 SLOTS = 6
 VMEM = pl.BlockSpec(memory_space=pltpu.VMEM)
-SMEM = pl.BlockSpec(memory_space=pltpu.SMEM)
+HBM = pl.BlockSpec(memory_space=pltpu.HBM)
 
 
 def split(value):
@@ -61,7 +61,7 @@
     return lax.axis_index("gx") * 3, lax.axis_index("gy") * 3
 
 
-def pack_kernel(mat_ref, rhs_ref, start_ref, out_ref):
+def pack(mat_ref, rhs_ref, start_ref, out_ref):
     flip_x, flip_y = flips()
     for y in range(4):
         for x in range(4):
@@ -76,6 +76,18 @@
                     out_ref[slot, 4 + p : 5 + p, :] = kind
 
 
+def pack_kernel(mat_hbm, rhs_hbm, start_hbm, out_ref, mat_ref, rhs_ref, start_ref, sems):
+    copies = [
+        pltpu.make_async_copy(source, target, sems.at[k])
+        for k, (source, target) in enumerate(((mat_hbm, mat_ref), (rhs_hbm, rhs_ref), (start_hbm, start_ref)))
+    ]
+    for copy in copies:
+        copy.start()
+    for copy in copies:
+        copy.wait()
+    pack(mat_ref, rhs_ref, start_ref, out_ref)
+
+
 def unpack_kernel(in_ref, forward_ref, backward_ref):
     flip_x, flip_y = flips()
     for y in range(4):
@@ -99,7 +111,7 @@
 def arrange_kernel(in_ref, rhs_ref, start_ref, kind_ref, mask_a_ref, mask_b_ref):
     for step in range(STEPS):
         for chunk in range(CHUNKS):
-            block, p = chunk * 4 + step // 2, step % 2
+            block, p = chunk * (STEPS // 2) + step // 2, step % 2
             row = step * CHUNKS + chunk
             rhs_ref[row : row + 1, :] = in_ref[block, p : p + 1, :]
             start_ref[row : row + 1, :] = in_ref[block, 2 + p : 3 + p, :]
@@ -124,8 +136,13 @@
             plain_ref[q, m] = joined[q * DOFS : (q + 1) * DOFS]
 
 
+def chain_order(descending):
+    steps, chunks = list(range(STEPS)), list(range(CHUNKS))
+    return (steps[::-1], chunks[::-1]) if descending else (steps, chunks)
+
+
 def maps_kernel(q, kind_ref, mask_a_ref, mask_b_ref, tables_ref, plain_ref, after_ref, map_ref, run_ref, wide_ref):
-    order = list(range(STEPS)) if q == 0 else list(reversed(range(STEPS)))
+    order = chain_order(q == 1)[0]
     for chunk in range(CHUNKS):
         row = order[0] * CHUNKS + chunk
         kind = jnp.broadcast_to(kind_ref[row : row + 1, :], (DOFS, LANES))
@@ -135,7 +152,7 @@
     for step in order[1:]:
         rows = pl.ds(step * CHUNKS, CHUNKS)
         mask_a, mask_b = mask_a_ref[rows, :], mask_b_ref[rows, :]
-        for group in range(4):
+        for group in range(CHUNKS // 4):
             for k in range(4):
                 chunk = group * 4 + k
                 a = jnp.broadcast_to(mask_a[chunk : chunk + 1, :], (DOFS, LANES))
@@ -144,17 +161,25 @@
             product = jnp.dot(wide_ref[...], tables_ref[q], preferred_element_type=F32)
             for k in range(4):
                 run_ref[group * 4 + k] = fold(product[k * 2 * DOFS : (k + 1) * 2 * DOFS])
-    for chunk in range(CHUNKS):
-        high, low = split(run_ref[chunk])
-        map_ref[chunk, :DOFS, :] = high
-        map_ref[chunk, DOFS:, :] = low
+    for place, chunk in enumerate(chain_order(q == 1)[1]):
+        product = run_ref[chunk]
+        if place % 2 == 1:
+            turned = product.T[:DOFS]
+            product = jnp.concatenate([turned, turned], axis=1)
+        map_ref[chunk] = product
+
+
+def both(mask):
+    return jnp.concatenate([mask, mask], axis=0)
+
+
+def pairs_of(state):
+    low = lax.broadcasted_iota(jnp.int32, (CHUNKS, LANES), 1) < DOFS
+    return jnp.where(low, state[:CHUNKS], state[CHUNKS:])
 
 
 def chain(const_ref, mask_a_ref, mask_b_ref, table_ref, map_ref, ends_ref, heads_ref, out_ref, descending):
-    steps = list(range(STEPS))
-    chunks = list(range(CHUNKS))
-    if descending:
-        steps, chunks = steps[::-1], chunks[::-1]
+    steps, chunks = chain_order(descending)
 
     def known(step):
         rows = pl.ds(step * CHUNKS, CHUNKS)
@@ -162,40 +187,36 @@
 
     def advance(state, step):
         rows = pl.ds(step * CHUNKS, CHUNKS)
-        a, b = mask_a_ref[rows, :], mask_b_ref[rows, :]
-        wide = widened(state, jnp.concatenate([a, a], axis=0), jnp.concatenate([b, b], axis=0))
+        wide = widened(state, both(mask_a_ref[rows, :]), both(mask_b_ref[rows, :]))
         product = jnp.dot(wide, table_ref[...], preferred_element_type=F32)
         return known(step) - fold(product)
 
     state = known(steps[0])
     for step in steps[1:]:
         state = advance(state, step)
-    ends_ref[...] = state
-
-    row = lax.broadcasted_iota(jnp.int32, (8, LANES), 0)
-    second = (row & 1) == 1
-    rest = (row & 2) == 2
-    head = jnp.zeros((8, LANES), F32)
-    for chunk in chunks:
-        heads_ref[chunk : chunk + 1, :] = head[0:1]
-        heads_ref[CHUNKS + chunk : CHUNKS + chunk + 1, :] = head[1:2]
-        if chunk == chunks[-1]:
-            break
-        high = head.astype(BF16).astype(F32)
-        wide = jnp.where(rest, head - high, high).astype(BF16)
-        product = jnp.dot(wide, map_ref[chunk], preferred_element_type=F32)
-        ends = jnp.where(
-            second,
-            jnp.broadcast_to(ends_ref[CHUNKS + chunk : CHUNKS + chunk + 1, :], (8, LANES)),
-            jnp.broadcast_to(ends_ref[chunk : chunk + 1, :], (8, LANES)),
-        )
-        head = (product + pltpu.roll(product, 2, 0)) + ends
-
-    low = lax.broadcasted_iota(jnp.int32, (CHUNKS, LANES), 1) < DOFS
-    state = heads_ref[...]
+    ends_ref[...] = pairs_of(state)
+
+    row = lax.broadcasted_iota(jnp.int32, (DOFS, LANES), 0)
+    lane = lax.broadcasted_iota(jnp.int32, (DOFS, LANES), 1)
+    low = lane < DOFS
+    unit = jnp.where((lane & (DOFS - 1)) == row, 1.0, 0.0)
+    upright = jnp.zeros((DOFS, LANES), F32)
+    for place, chunk in enumerate(chunks):
+        end = ends_ref[chunk : chunk + 1, :]
+        if place % 2 == 0:
+            heads_ref[chunk : chunk + 1, :] = jnp.sum(upright * unit, axis=0, keepdims=True)
+            flat = jnp.sum(upright * map_ref[chunk], axis=0, keepdims=True) + end
+        else:
+            heads_ref[chunk : chunk + 1, :] = flat
+            terms = flat * map_ref[chunk] + end * unit
+            first = jnp.sum(jnp.where(low, terms, 0.0), axis=1, keepdims=True)
+            second = jnp.sum(jnp.where(low, 0.0, terms), axis=1, keepdims=True)
+            upright = jnp.where(low, first, second)
+
+    state = doubled(heads_ref[...])
     for step in steps:
         state = advance(state, step)
-        out_ref[pl.ds(step * CHUNKS, CHUNKS), :] = jnp.where(low, state[:CHUNKS], state[CHUNKS:])
+        out_ref[pl.ds(step * CHUNKS, CHUNKS), :] = pairs_of(state)
 
 
 def beside_inside(refs):
@@ -214,10 +235,6 @@
         product = jnp.dot(wide_ref[:, k * 256 : (k + 1) * 256], tables_ref[first + k], preferred_element_type=F32)
         total = product if total is None else total + product
     return fold(total)
-
-
-def both(mask):
-    return jnp.concatenate([mask, mask], axis=0)
 
 
 def forward_kernel(rhs_ref, start_ref, n0_ref, n1_ref, n2_ref, n3_ref, mask_a_ref, mask_b_ref, tables_ref,
@@ -243,7 +260,7 @@
     chain(const_ref, mask_a_ref, mask_b_ref, tables_ref.at[1], map_ref, ends_ref, heads_ref, backward_ref, True)
     for step in range(STEPS):
         for chunk in range(CHUNKS):
-            block, p = chunk * 4 + step // 2, step % 2
+            block, p = chunk * (STEPS // 2) + step // 2, step % 2
             row = step * CHUNKS + chunk
             out_ref[block, p : p + 1, :] = forward_ref[row : row + 1, :]
             out_ref[block, 2 + p : 3 + p, :] = backward_ref[row : row + 1, :]
@@ -255,7 +272,7 @@
     return jax.ShapeDtypeStruct(dims, dtype)
 
 
-def call(kernel, outs, ins, scratch=(), flops=1000000):
+def call(kernel, outs, ins, scratch=(), flops=1000000, limit=16 * 1024 * 1024):
     return pl.pallas_call(
         kernel,
         out_shape=outs,
@@ -263,7 +280,7 @@
         out_specs=jax.tree.map(lambda _: VMEM, outs),
         scratch_shapes=scratch,
         cost_estimate=pl.CostEstimate(flops=flops, bytes_accessed=500000, transcendentals=0),
-        compiler_params=pltpu.CompilerParams(vmem_limit_bytes=16 * 1024 * 1024),
+        compiler_params=pltpu.CompilerParams(vmem_limit_bytes=limit),
     )
 
 
@@ -288,7 +305,18 @@
 def per_device(rhs_field, start_field, material, diag_inverse, z_blocks, side_blocks):
     mask = shape(ROWS, LANES, dtype=BF16)
     field = shape(ROWS, LANES)
-    packed = call(pack_kernel, shape(PEERS, SLOTS, LANES), [SMEM, VMEM, VMEM])(material, rhs_field, start_field)
+    packed = call(
+        pack_kernel,
+        shape(PEERS, SLOTS, LANES),
+        [HBM] * 3,
+        [
+            pltpu.SMEM(material.shape, jnp.int32),
+            pltpu.VMEM(rhs_field.shape, F32),
+            pltpu.VMEM(rhs_field.shape, F32),
+            pltpu.SemaphoreType.DMA((3,)),
+        ],
+        limit=None,
+    )(material, rhs_field, start_field)
     arrived = lax.all_to_all(packed, GZ, 0, 0, tiled=True)
     tables, plain = call(
         tables_kernel,
@@ -302,7 +330,7 @@
     def maps(q, after):
         return call(
             functools.partial(maps_kernel, q),
-            shape(CHUNKS, 2 * DOFS, LANES, dtype=BF16),
+            shape(CHUNKS, DOFS, LANES),
             [VMEM] * 5 + [pl.BlockSpec(memory_space=pl.ANY)],
             [pltpu.VMEM((CHUNKS, DOFS, LANES), F32), pltpu.VMEM((8 * DOFS, 256), BF16)],
             flops=4000000000,
@@ -311,8 +339,8 @@
     map_f = maps(0, start)
     chain_scratch = [
         pltpu.VMEM((2 * ROWS, LANES), F32),
-        pltpu.VMEM((2 * CHUNKS, LANES), F32),
-        pltpu.VMEM((2 * CHUNKS, LANES), F32),
+        pltpu.VMEM((CHUNKS, LANES), F32),
+        pltpu.VMEM((CHUNKS, LANES), F32),
     ]
     forward, given = call(
         forward_kernel,

time: 76.3 us -> 71.9 us (0.942)
  local copies, waits for them, and re-layouts: 2.37 us -> 0.02 us
  Pallas kernels: 16.3 us -> 14.1 us
    unnamed x12 -> x6, local copies, waits for them, and re-layouts: 2.37 us -> 0.02 us
    pallas_call x1, Pallas kernels: 4.49 us -> 3.32 us  [per_device(): call(forward_kernel, (field, shape(2 * ROWS, LANES)), [VMEM] * 10, chain_...]
    pallas_call x1, Pallas kernels: 4.42 us -> 3.32 us  [per_device(): call(backward_kernel, shape(PEERS, SLOTS, LANES), [VMEM] * 10, chain_scra...]
where the time goes in v2:
time: 71.9 us; the launch traced here: 71.7 us
  starting transfers between devices  22.9 us (32%)
  blocking collectives  18.9 us (26%)
  waiting for transfers between devices  15 us (21%)
  Pallas kernels  14.1 us (20%)
  between operations  0.78 us (1%)
    all_to_all x1, blocking collectives, per_device(): returned = lax.all_to_all(ready, GZ, 0, 0, tiled=True)  18.9 us
    all_to_all x1, starting transfers between devices, per_device(): arrived = lax.all_to_all(packed, GZ, 0, 0, tiled=True)  14.8 us
    all_to_all x1, waiting for transfers between devices, per_device(): arrived = lax.all_to_all(packed, GZ, 0, 0, tiled=True)  12.5 us
    ppermute x8, starting transfers between devices, moved(): return lax.ppermute(value, axes, pairs)  8.13 us
    pallas_call x2, Pallas kernels, maps(): call(functools.partial(maps_kernel, q), shape(CHUNKS, DOFS, LANES), [VMEM...  3.98 us
    pallas_call x1, Pallas kernels, per_device(): call(forward_kernel, (field, shape(2 * ROWS, LANES)), [VMEM] * 10, chain_...  3.32 us
    pallas_call x1, Pallas kernels, per_device(): call(backward_kernel, shape(PEERS, SLOTS, LANES), [VMEM] * 10, chain_scra...  3.32 us
    ppermute x8, waiting for transfers between devices, moved(): return lax.ppermute(value, axes, pairs)  2.48 us
  transfers between devices with their start and end apart: 9, of which 5 were waited for; matrix products, arithmetic and copies ran while one was open for 0% of the time, Pallas kernels for 7%

profile of v2, /device:TPU:2, one launch (start us, length us, event | category | flops | bytes accessed | tf_op | source)
XLA Modules:
  0.0 71.7 jit_solution(5884242536757150713)
XLA Ops:
  0.6 1.8 %shard_map.77 = f32[64,6,128]{2,1,0:T(8,128)} custom-call(s32[2,4,4]{2,1,0:T(4,128)} %mat_hbm.1, f32[2,4,4,512]{3,2,1,0:T(4,128)} %rhs_hbm.1, f32[2,4,4,512]{3,2,1,0:T(4,128)} %start_hbm.1), custom_call_target="tpu_custom_call" | custom-call | flops 1000000 | bytes 500000 | tf_op jit(solution)/shard_map/pallas_call | solution.py:308
  2.4 0.0 copy-start.2
  2.4 14.8 %all-to-all-start = ((f32[64,6,128]{2,1,0:T(8,128)}), f32[64,6,128]{2,1,0:T(8,128)S(1)}, u32[]{:S(2)}, u32[]{:S(2)}) async-start(f32[64,6,128]{2,1,0:T(8,128)} %shard_map.77), calls=%async_computation | async-start | bytes 524288 | tf_op jit(solution)/shard_map/all_to_all | solution.py:320
  17.3 0.9 %shard_map.79 = (bf16[7,256,256]{2,1,0:T(8,128)(2,1)S(1)}, f32[2,4,64,128]{3,2,1,0:T(8,128)S(1)}) custom-call(f32[4,64,64]{2,1,0:T(8,128)S(1)} %copy-done.2, f32[4,2,64,64]{3,2,1,0:T(8,128)S(1)} %copy-done.1, f32[4,4,64,64]{3,2,1,0:T(8,128)S(1)} %copy-done), custom_call_target="tpu_custom_call" | custom-call | flops 4000000000 | bytes 500000 | tf_op jit(solution)/shard_map/pallas_call | solution.py:321
  18.1 12.5 %all-to-all-done.in_ref = f32[64,6,128]{2,1,0:T(8,128)S(1)} async-done(((f32[64,6,128]{2,1,0:T(8,128)}), f32[64,6,128]{2,1,0:T(8,128)S(1)}, u32[]{:S(2)}, u32[]{:S(2)}) %all-to-all-start) | async-done | bytes 196640 | tf_op jit(solution)/shard_map/all_to_all | solution.py:320
  30.6 0.2 shard_map.78
  30.8 1.5 %collective-permute-start.3 = (f32[128,128]{1,0:T(8,128)S(1)}, f32[128,128]{1,0:T(8,128)S(1)}, u32[]{:S(2)}, u32[]{:S(2)}) collective-permute-start(f32[128,128]{1,0:T(8,128)S(1)} %get-tuple-element.12.after_ref.start_ref), channel_id=1, source_target_pairs={{0,2},{8,0},{16,8},{24,16},{26,24},{18,26},{10,18},{2,10},{1,3},{9... | collective-permute-start | bytes 196616 | tf_op jit(solution)/shard_map/ppermute | solution.py:293
  32.3 0.5 collective-permute-start.2
  32.8 0.7 collective-permute-start.1
  33.5 1.3 %collective-permute-start = (f32[128,128]{1,0:T(8,128)S(1)}, f32[128,128]{1,0:T(8,128)S(1)}, u32[]{:S(2)}, u32[]{:S(2)}) collective-permute-start(f32[128,128]{1,0:T(8,128)S(1)} %get-tuple-element.12.after_ref.start_ref), channel_id=1, source_target_pairs={{0,32},{32,64},{64,96},{96,97},{97,65},{65,33},{33,1},{1,0},{2,34}... | collective-permute-start | bytes 196616 | tf_op jit(solution)/shard_map/ppermute | solution.py:293
  34.9 2.0 %shard_map.80.map_ref = f32[32,64,128]{2,1,0:T(8,128)S(1)} custom-call(f32[128,128]{1,0:T(8,128)S(1)} %get-tuple-element.16.kind_ref, bf16[128,128]{1,0:T(8,128)(2,1)S(1)} %get-tuple-element.13.mask_a_ref, bf16[128,128]{1,0:T(8,128)(2,1)S(1)} %get-tuple-element.14.mask_b_ref, bf16[7,256,256]{2,1,0:T(8,128)(2,1)S(1)} %get-tuple-element.15.tables_ref, ...), custom_call_target="tpu_custom_call" | custom-call | flops 4000000000 | bytes 500000 | tf_op jit(solution)/shard_map/pallas_call | solution.py:331
  36.9 0.2 collective-permute-done.1.n1_ref
  37.1 0.7 collective-permute-done.n0_ref
  37.8 3.3 %shard_map.81 = (f32[128,128]{1,0:T(8,128)S(1)}, f32[256,128]{1,0:T(8,128)S(1)}) custom-call(f32[128,128]{1,0:T(8,128)S(1)} %get-tuple-element.11.rhs_ref, f32[128,128]{1,0:T(8,128)S(1)} %get-tuple-element.12.after_ref.start_ref, f32[128,128]{1,0:T(8,128)S(1)} %collective-permute-done.n0_ref, f32[128,128]{1,0:T(8,128)S(1)} %collective-permute-done.1.n1_ref, ...), custom_call_target="tpu_custom_call" | custom-call | flops 4000000000 | bytes 500000 | tf_op jit(solution)/shard_map/pallas_call | solution.py:345
  41.1 1.5 %collective-permute-start.7 = (f32[128,128]{1,0:T(8,128)S(1)}, f32[128,128]{1,0:T(8,128)S(1)}, u32[]{:S(2)}, u32[]{:S(2)}) collective-permute-start(f32[128,128]{1,0:T(8,128)S(1)} %get-tuple-element.18.after_ref.forward_ref), channel_id=1, source_target_pairs={{0,2},{8,0},{16,8},{24,16},{26,24},{18,26},{10,18},{2,10},{1,3},{9... | collective-permute-start | bytes 196616 | tf_op jit(solution)/shard_map/ppermute | solution.py:293
  42.6 0.5 collective-permute-start.6
  43.2 1.3 %collective-permute-start.5 = (f32[128,128]{1,0:T(8,128)S(1)}, f32[128,128]{1,0:T(8,128)S(1)}, u32[]{:S(2)}, u32[]{:S(2)}) collective-permute-start(f32[128,128]{1,0:T(8,128)S(1)} %get-tuple-element.18.after_ref.forward_ref), channel_id=1, source_target_pairs={{0,1},{32,0},{64,32},{96,64},{97,96},{65,97},{33,65},{1,33},{2,3},... | collective-permute-start | bytes 196616 | tf_op jit(solution)/shard_map/ppermute | solution.py:293
  44.5 0.7 collective-permute-start.4
  45.2 2.0 %shard_map.82.map_ref = f32[32,64,128]{2,1,0:T(8,128)S(1)} custom-call(f32[128,128]{1,0:T(8,128)S(1)} %get-tuple-element.16.kind_ref, bf16[128,128]{1,0:T(8,128)(2,1)S(1)} %get-tuple-element.13.mask_a_ref, bf16[128,128]{1,0:T(8,128)(2,1)S(1)} %get-tuple-element.14.mask_b_ref, bf16[7,256,256]{2,1,0:T(8,128)(2,1)S(1)} %get-tuple-element.15.tables_ref, ...), custom_call_target="tpu_custom_call" | custom-call | flops 4000000000 | bytes 500000 | tf_op jit(solution)/shard_map/pallas_call | solution.py:331
  47.2 0.3 collective-permute-done.5.n1_ref
  47.4 1.3 %collective-permute-done.4.n0_ref = f32[128,128]{1,0:T(8,128)S(1)} collective-permute-done((f32[128,128]{1,0:T(8,128)S(1)}, f32[128,128]{1,0:T(8,128)S(1)}, u32[]{:S(2)}, u32[]{:S(2)}) %collective-permute-start.4) | collective-permute-done | bytes 65568 | tf_op jit(solution)/shard_map/ppermute | solution.py:293
  48.8 3.3 %shard_map.83 = f32[64,6,128]{2,1,0:T(8,128)S(1)} custom-call(f32[128,128]{1,0:T(8,128)S(1)} %get-tuple-element.18.after_ref.forward_ref, f32[256,128]{1,0:T(8,128)S(1)} %get-tuple-element.19.given_ref, f32[128,128]{1,0:T(8,128)S(1)} %collective-permute-done.4.n0_ref, f32[128,128]{1,0:T(8,128)S(1)} %collective-permute-done.5.n1_ref, ...), custom_call_target="tpu_custom_call" | custom-call | flops 4000000000 | bytes 500000 | tf_op jit(solution)/shard_map/pallas_call | solution.py:355
  52.1 18.9 %all_to_all.10.in_ref = f32[64,6,128]{2,1,0:T(8,128)S(1)} all-to-all(f32[64,6,128]{2,1,0:T(8,128)S(1)} %shard_map.83), channel_id=1, replica_groups=mesh['ah'=2,'am'=2,'al'=2,'b'=4,'c'=2,'gx'=2,'gy'=2] {'ah','am','al','b'..., dimensions={0} | all-to-all | bytes 393216 | tf_op jit(solution)/shard_map/all_to_all | solution.py:362
  71.0 0.7 %shard_map.84 = (f32[2,4,4,512]{3,2,1,0:T(4,128)}, f32[2,4,4,512]{3,2,1,0:T(4,128)}) custom-call(f32[64,6,128]{2,1,0:T(8,128)S(1)} %all_to_all.10.in_ref), custom_call_target="tpu_custom_call" | custom-call | flops 1000000 | bytes 500000 | tf_op jit(solution)/shard_map/pallas_call | solution.py:364
  (9 shorter events, 0.0 us)
Async XLA Ops:
  0.6 16.6 %copy-start = (f32[4,4,64,64]{3,2,1,0:T(8,128)S(1)}, f32[4,4,64,64]{3,2,1,0:T(8,128)}, u32[]{:S(2)}) copy-start(f32[4,4,64,64]{3,2,1,0:T(8,128)} %side_ref.1) | copy-start | bytes 786436
  2.4 14.8 %copy-start.1 = (f32[4,2,64,64]{3,2,1,0:T(8,128)S(1)}, f32[4,2,64,64]{3,2,1,0:T(8,128)}, u32[]{:S(2)}) copy-start(f32[4,2,64,64]{3,2,1,0:T(8,128)} %z_ref.1) | copy-start | bytes 393220
  2.4 14.8 %copy-start.2 = (f32[4,64,64]{2,1,0:T(8,128)S(1)}, f32[4,64,64]{2,1,0:T(8,128)}, u32[]{:S(2)}) copy-start(f32[4,64,64]{2,1,0:T(8,128)} %diag_ref.1) | copy-start | bytes 196612
  2.4 28.2 %all-to-all-start = ((f32[64,6,128]{2,1,0:T(8,128)}), f32[64,6,128]{2,1,0:T(8,128)S(1)}, u32[]{:S(2)}, u32[]{:S(2)}) async-start(f32[64,6,128]{2,1,0:T(8,128)} %shard_map.77), calls=%async_computation | async-start | bytes 524288 | tf_op jit(solution)/shard_map/all_to_all | solution.py:320
  30.8 6.1 %collective-permute-start.3 = (f32[128,128]{1,0:T(8,128)S(1)}, f32[128,128]{1,0:T(8,128)S(1)}, u32[]{:S(2)}, u32[]{:S(2)}) collective-permute-start(f32[128,128]{1,0:T(8,128)S(1)} %get-tuple-element.12.after_ref.start_ref), channel_id=1, source_target_pairs={{0,2},{8,0},{16,8},{24,16},{26,24},{18,26},{10,18},{2,10},{1,3},{9... | collective-permute-start | bytes 196616 | tf_op jit(solution)/shard_map/ppermute | solution.py:293
  32.3 4.6 %collective-permute-start.2 = (f32[128,128]{1,0:T(8,128)S(1)}, f32[128,128]{1,0:T(8,128)S(1)}, u32[]{:S(2)}, u32[]{:S(2)}) collective-permute-start(f32[128,128]{1,0:T(8,128)S(1)} %get-tuple-element.12.after_ref.start_ref), channel_id=1, source_target_pairs={{0,8},{8,16},{16,24},{24,26},{26,18},{18,10},{10,2},{2,0},{1,9},{9... | collective-permute-start | bytes 196616 | tf_op jit(solution)/shard_map/ppermute | solution.py:293
  32.8 4.3 %collective-permute-start.1 = (f32[128,128]{1,0:T(8,128)S(1)}, f32[128,128]{1,0:T(8,128)S(1)}, u32[]{:S(2)}, u32[]{:S(2)}) collective-permute-start(f32[128,128]{1,0:T(8,128)S(1)} %get-tuple-element.12.after_ref.start_ref), channel_id=1, source_target_pairs={{0,1},{32,0},{64,32},{96,64},{97,96},{65,97},{33,65},{1,33},{2,3},... | collective-permute-start | bytes 196616 | tf_op jit(solution)/shard_map/ppermute | solution.py:293
  33.5 4.3 %collective-permute-start = (f32[128,128]{1,0:T(8,128)S(1)}, f32[128,128]{1,0:T(8,128)S(1)}, u32[]{:S(2)}, u32[]{:S(2)}) collective-permute-start(f32[128,128]{1,0:T(8,128)S(1)} %get-tuple-element.12.after_ref.start_ref), channel_id=1, source_target_pairs={{0,32},{32,64},{64,96},{96,97},{97,65},{65,33},{33,1},{1,0},{2,34}... | collective-permute-start | bytes 196616 | tf_op jit(solution)/shard_map/ppermute | solution.py:293
  41.1 6.0 %collective-permute-start.7 = (f32[128,128]{1,0:T(8,128)S(1)}, f32[128,128]{1,0:T(8,128)S(1)}, u32[]{:S(2)}, u32[]{:S(2)}) collective-permute-start(f32[128,128]{1,0:T(8,128)S(1)} %get-tuple-element.18.after_ref.forward_ref), channel_id=1, source_target_pairs={{0,2},{8,0},{16,8},{24,16},{26,24},{18,26},{10,18},{2,10},{1,3},{9... | collective-permute-start | bytes 196616 | tf_op jit(solution)/shard_map/ppermute | solution.py:293
  42.6 4.5 %collective-permute-start.6 = (f32[128,128]{1,0:T(8,128)S(1)}, f32[128,128]{1,0:T(8,128)S(1)}, u32[]{:S(2)}, u32[]{:S(2)}) collective-permute-start(f32[128,128]{1,0:T(8,128)S(1)} %get-tuple-element.18.after_ref.forward_ref), channel_id=1, source_target_pairs={{0,8},{8,16},{16,24},{24,26},{26,18},{18,10},{10,2},{2,0},{1,9},{9... | collective-permute-start | bytes 196616 | tf_op jit(solution)/shard_map/ppermute | solution.py:293
  43.2 4.3 %collective-permute-start.5 = (f32[128,128]{1,0:T(8,128)S(1)}, f32[128,128]{1,0:T(8,128)S(1)}, u32[]{:S(2)}, u32[]{:S(2)}) collective-permute-start(f32[128,128]{1,0:T(8,128)S(1)} %get-tuple-element.18.after_ref.forward_ref), channel_id=1, source_target_pairs={{0,1},{32,0},{64,32},{96,64},{97,96},{65,97},{33,65},{1,33},{2,3},... | collective-permute-start | bytes 196616 | tf_op jit(solution)/shard_map/ppermute | solution.py:293
  44.5 4.3 %collective-permute-start.4 = (f32[128,128]{1,0:T(8,128)S(1)}, f32[128,128]{1,0:T(8,128)S(1)}, u32[]{:S(2)}, u32[]{:S(2)}) collective-permute-start(f32[128,128]{1,0:T(8,128)S(1)} %get-tuple-element.18.after_ref.forward_ref), channel_id=1, source_target_pairs={{0,32},{32,64},{64,96},{96,97},{97,65},{65,33},{33,1},{1,0},{2,34}... | collective-permute-start | bytes 196616 | tf_op jit(solution)/shard_map/ppermute | solution.py:293

commit v3 on v2

--- a/solution.py
+++ b/solution.py
@@ -20,7 +20,7 @@
 CHUNKS = 128 // STEPS
 ROWS = STEPS * CHUNKS
 PEERS = 64
-SLOTS = 6
+SLOTS = 5
 VMEM = pl.BlockSpec(memory_space=pltpu.VMEM)
 HBM = pl.BlockSpec(memory_space=pltpu.HBM)
 
@@ -63,17 +63,19 @@
 
 def pack(mat_ref, rhs_ref, start_ref, out_ref):
     flip_x, flip_y = flips()
+    low = lax.broadcasted_iota(jnp.int32, (1, LANES), 1) < DOFS
     for y in range(4):
         for x in range(4):
             block = block_of(y, x, flip_y, flip_x)
+            kinds = jnp.where(low, mat_ref[0, y, x].astype(F32), mat_ref[1, y, x].astype(F32))
+            for part in range(4):
+                out_ref[block + (part // 2) * 32 + part % 2, 4:5, :] = kinds
             for p in range(2):
-                kind = jnp.full((1, LANES), mat_ref[p, y, x].astype(F32))
                 for part in range(4):
                     lanes = slice(part * LANES, (part + 1) * LANES)
                     slot = block + (part // 2) * 32 + part % 2
                     out_ref[slot, p : p + 1, :] = rhs_ref[p, y, x : x + 1, lanes]
                     out_ref[slot, 2 + p : 3 + p, :] = start_ref[p, y, x : x + 1, lanes]
-                    out_ref[slot, 4 + p : 5 + p, :] = kind
 
 
 def pack_kernel(mat_hbm, rhs_hbm, start_hbm, out_ref, mat_ref, rhs_ref, start_ref, sems):
@@ -115,25 +117,38 @@
             row = step * CHUNKS + chunk
             rhs_ref[row : row + 1, :] = in_ref[block, p : p + 1, :]
             start_ref[row : row + 1, :] = in_ref[block, 2 + p : 3 + p, :]
-            kind_ref[row : row + 1, :] = in_ref[block, 4 + p : 5 + p, :]
+            kind_ref[row : row + 1, :] = in_ref[block, 4:5, :]
+    kinds = kind_ref[...]
+    low = lax.broadcasted_iota(jnp.int32, kinds.shape, 1) < DOFS
+    odd = (lax.broadcasted_iota(jnp.int32, kinds.shape, 0) // CHUNKS) % 2 == 1
+    kind_ref[...] = jnp.where(low == odd, pltpu.roll(kinds, DOFS, 1), kinds)
     mask_a, mask_b = masks_of(kind_ref[...])
     mask_a_ref[...] = mask_a
     mask_b_ref[...] = mask_b
 
 
-def tables_kernel(diag_ref, z_ref, side_ref, tables_ref, plain_ref):
+def tables_kernel(diag_ref, z_ref, side_ref, tables_ref, sides_ref, own_ref, plain_ref):
+    low_half = lax.broadcasted_iota(jnp.int32, (7 * DOFS, LANES), 1) < DOFS
+    joined = []
     for m in range(KINDS):
         inverse = jnp.concatenate([diag_ref[m], diag_ref[m]], axis=1)
         left = jnp.concatenate([z_ref[m].reshape(2 * DOFS, DOFS), side_ref[m].reshape(4 * DOFS, DOFS)], axis=0)
-        joined = jnp.dot(left, inverse, precision=HIGH, preferred_element_type=F32)
-        joined = jnp.concatenate([joined, inverse], axis=0)
-        high, low = split(joined)
-        for q in range(7):
-            rows = slice(q * DOFS, (q + 1) * DOFS)
-            tables_ref[q, m * DOFS : (m + 1) * DOFS, :LANES] = high[rows]
-            tables_ref[q, m * DOFS : (m + 1) * DOFS, LANES:] = low[rows]
+        product = jnp.dot(left, inverse, precision=HIGH, preferred_element_type=F32)
         for q in range(2):
-            plain_ref[q, m] = joined[q * DOFS : (q + 1) * DOFS]
+            part = product[q * DOFS : (q + 1) * DOFS]
+            plain_ref[q, m] = part
+            high, low = split(part)
+            tables_ref[q, m * DOFS : (m + 1) * DOFS, :LANES] = high
+            tables_ref[q, m * DOFS : (m + 1) * DOFS, LANES:] = low
+        joined.append(jnp.concatenate([product, inverse], axis=0))
+    for half in range(2):
+        lanes = slice(half * LANES, (half + 1) * LANES)
+        high, low = split(jnp.where(low_half, joined[2 * half], joined[2 * half + 1]))
+        sides_ref[0, :, lanes] = high[2 * DOFS : 6 * DOFS]
+        sides_ref[1, :, lanes] = low[2 * DOFS : 6 * DOFS]
+        for k, q in enumerate((1, 6)):
+            own_ref[k, :DOFS, lanes] = high[q * DOFS : (q + 1) * DOFS]
+            own_ref[k, DOFS:, lanes] = low[q * DOFS : (q + 1) * DOFS]
 
 
 def chain_order(descending):
@@ -227,35 +242,56 @@
     return [jnp.where(here, ref[...], 0.0) for here, ref in zip(inside, refs)]
 
 
-def neighbour_terms(wide_ref, pieces, mask_a, mask_b, tables_ref, first):
-    for k, piece in enumerate(pieces):
-        wide_ref[:, k * 256 : (k + 1) * 256] = widened(doubled(piece), mask_a, mask_b)
-    total = None
-    for k in range(len(pieces)):
-        product = jnp.dot(wide_ref[:, k * 256 : (k + 1) * 256], tables_ref[first + k], preferred_element_type=F32)
-        total = product if total is None else total + product
-    return fold(total)
+def stacked(value):
+    high, low = split(value)
+    return jnp.concatenate([high, low], axis=0)
+
+
+def beside_each_other(first, second):
+    low = lax.broadcasted_iota(jnp.int32, first.shape, 1) < DOFS
+    return jnp.concatenate(
+        [jnp.where(low, first, pltpu.roll(second, DOFS, 1)), jnp.where(low, pltpu.roll(first, DOFS, 1), second)], axis=0
+    )
+
+
+def product_of(left, pair_ref):
+    total = jnp.dot(left, pair_ref[0], preferred_element_type=F32)
+    return total + jnp.dot(left, pair_ref[1], preferred_element_type=F32)
+
+
+def chosen(product, mask_a, mask_b):
+    rows = product.shape[0] // 2
+    total = product[:rows] + product[rows:]
+    kept = total[:, :LANES] * mask_a + total[:, LANES:] * mask_b
+    return kept + pltpu.roll(kept, DOFS, 1)
+
+
+def side_product(pieces, sides_ref):
+    left = jnp.concatenate([beside_each_other(*pieces[:2]), beside_each_other(*pieces[2:])], axis=1)
+    return product_of(stacked(left), sides_ref)
+
+
+def own_product(piece, pair_ref):
+    return jnp.dot(stacked(doubled(piece)), pair_ref[...], preferred_element_type=F32)
 
 
 def forward_kernel(rhs_ref, start_ref, n0_ref, n1_ref, n2_ref, n3_ref, mask_a_ref, mask_b_ref, tables_ref,
-                   map_ref, forward_ref, given_ref, const_ref, ends_ref, heads_ref, wide_ref):
-    mask_a, mask_b = both(mask_a_ref[...]), both(mask_b_ref[...])
+                   sides_ref, own_ref, map_ref, forward_ref, given_ref, const_ref, ends_ref, heads_ref):
+    mask_a, mask_b = both(mask_a_ref[...].astype(F32)), both(mask_b_ref[...].astype(F32))
     start = start_ref[...]
     following = jnp.concatenate([start[1:CHUNKS], jnp.zeros((1, LANES), F32)], axis=0)
     upper = jnp.concatenate([start[CHUNKS:], following], axis=0)
-    pieces = [upper] + beside_inside((n0_ref, n1_ref, n2_ref, n3_ref))
-    given = neighbour_terms(wide_ref, pieces, mask_a, mask_b, tables_ref, 1)
+    product = side_product(beside_inside((n0_ref, n1_ref, n2_ref, n3_ref)), sides_ref)
+    given = chosen(product + own_product(upper, own_ref.at[0]), mask_a, mask_b)
     given_ref[...] = given
-    own = widened(doubled(rhs_ref[...]), mask_a, mask_b)
-    const_ref[...] = fold(jnp.dot(own, tables_ref[6], preferred_element_type=F32)) - given
+    const_ref[...] = chosen(own_product(rhs_ref[...], own_ref.at[1]), mask_a, mask_b) - given
     chain(const_ref, mask_a_ref, mask_b_ref, tables_ref.at[0], map_ref, ends_ref, heads_ref, forward_ref, False)
 
 
-def backward_kernel(forward_ref, given_ref, n0_ref, n1_ref, n2_ref, n3_ref, mask_a_ref, mask_b_ref,
-                    tables_ref, map_ref, out_ref, const_ref, ends_ref, heads_ref, wide_ref, backward_ref):
-    mask_a, mask_b = both(mask_a_ref[...]), both(mask_b_ref[...])
-    pieces = beside_inside((n0_ref, n1_ref, n2_ref, n3_ref))
-    terms = neighbour_terms(wide_ref, pieces, mask_a, mask_b, tables_ref, 2)
+def backward_kernel(forward_ref, given_ref, n0_ref, n1_ref, n2_ref, n3_ref, mask_a_ref, mask_b_ref, tables_ref,
+                    sides_ref, map_ref, out_ref, const_ref, ends_ref, heads_ref, backward_ref):
+    mask_a, mask_b = both(mask_a_ref[...].astype(F32)), both(mask_b_ref[...].astype(F32))
+    terms = chosen(side_product(beside_inside((n0_ref, n1_ref, n2_ref, n3_ref)), sides_ref), mask_a, mask_b)
     const_ref[...] = doubled(forward_ref[...]) + (given_ref[...] - terms)
     chain(const_ref, mask_a_ref, mask_b_ref, tables_ref.at[1], map_ref, ends_ref, heads_ref, backward_ref, True)
     for step in range(STEPS):
@@ -264,8 +300,6 @@
             row = step * CHUNKS + chunk
             out_ref[block, p : p + 1, :] = forward_ref[row : row + 1, :]
             out_ref[block, 2 + p : 3 + p, :] = backward_ref[row : row + 1, :]
-    for block in range(PEERS):
-        out_ref[block, 4:6, :] = jnp.zeros((2, LANES), F32)
 
 
 def shape(*dims, dtype=F32):
@@ -318,9 +352,10 @@
         limit=None,
     )(material, rhs_field, start_field)
     arrived = lax.all_to_all(packed, GZ, 0, 0, tiled=True)
-    tables, plain = call(
+    square = shape(2, 256, 256, dtype=BF16)
+    tables, sides, own, plain = call(
         tables_kernel,
-        (shape(7, 256, 256, dtype=BF16), shape(2, KINDS, DOFS, LANES)),
+        (square, square, shape(2, 2 * DOFS, 256, dtype=BF16), shape(2, KINDS, DOFS, LANES)),
         [VMEM] * 3,
         flops=4000000000,
     )(diag_inverse, z_blocks, side_blocks)
@@ -345,20 +380,20 @@
     forward, given = call(
         forward_kernel,
         (field, shape(2 * ROWS, LANES)),
-        [VMEM] * 10,
-        chain_scratch + [pltpu.VMEM((4 * ROWS, 5 * 256), BF16)],
+        [VMEM] * 12,
+        chain_scratch,
         flops=4000000000,
-    )(rhs, start, *beside, mask_a, mask_b, tables, map_f)
+    )(rhs, start, *beside, mask_a, mask_b, tables, sides, own, map_f)
 
     beside = neighbours(forward)
     map_b = maps(1, forward)
     ready = call(
         backward_kernel,
-        shape(PEERS, SLOTS, LANES),
-        [VMEM] * 10,
-        chain_scratch + [pltpu.VMEM((4 * ROWS, 4 * 256), BF16), pltpu.VMEM((ROWS, LANES), F32)],
+        shape(PEERS, 4, LANES),
+        [VMEM] * 11,
+        chain_scratch + [pltpu.VMEM((ROWS, LANES), F32)],
         flops=4000000000,
-    )(forward, given, *beside, mask_a, mask_b, tables, map_b)
+    )(forward, given, *beside, mask_a, mask_b, tables, sides, map_b)
     returned = lax.all_to_all(ready, GZ, 0, 0, tiled=True)
     cells = shape(*rhs_field.shape)
     return call(unpack_kernel, (cells, cells), [VMEM])(returned)

time: 71.9 us -> 71.1 us (0.989)
  no operation moved by 1% of the time
where the time goes in v3:
time: 71.1 us; the launch traced here: 70.9 us
  starting transfers between devices  22.9 us (32%)
  blocking collectives  18.2 us (26%)
  waiting for transfers between devices  15 us (21%)
  Pallas kernels  14 us (20%)
  between operations  0.78 us (1%)
    all_to_all x1, blocking collectives, per_device(): returned = lax.all_to_all(ready, GZ, 0, 0, tiled=True)  18.2 us
    all_to_all x1, starting transfers between devices, per_device(): arrived = lax.all_to_all(packed, GZ, 0, 0, tiled=True)  14.8 us
    all_to_all x1, waiting for transfers between devices, per_device(): arrived = lax.all_to_all(packed, GZ, 0, 0, tiled=True)  12.5 us
    ppermute x8, starting transfers between devices, moved(): return lax.ppermute(value, axes, pairs)  8.13 us
    pallas_call x2, Pallas kernels, maps(): call(functools.partial(maps_kernel, q), shape(CHUNKS, DOFS, LANES), [VMEM...  3.98 us
    pallas_call x1, Pallas kernels, per_device(): call(forward_kernel, (field, shape(2 * ROWS, LANES)), [VMEM] * 12, chain_...  3.29 us
    pallas_call x1, Pallas kernels, per_device(): call(backward_kernel, shape(PEERS, 4, LANES), [VMEM] * 11, chain_scratch...  3.25 us
    ppermute x8, waiting for transfers between devices, moved(): return lax.ppermute(value, axes, pairs)  2.48 us
  transfers between devices with their start and end apart: 9, of which 5 were waited for; matrix products, arithmetic and copies ran while one was open for 0% of the time, Pallas kernels for 7%

profile of v3, /device:TPU:2, one launch (start us, length us, event | category | flops | bytes accessed | tf_op | source)
XLA Modules:
  0.0 70.9 jit_solution(12438619769386190338)
XLA Ops:
  0.6 1.8 %shard_map.77 = f32[64,5,128]{2,1,0:T(8,128)} custom-call(s32[2,4,4]{2,1,0:T(4,128)} %mat_hbm.1, f32[2,4,4,512]{3,2,1,0:T(4,128)} %rhs_hbm.1, f32[2,4,4,512]{3,2,1,0:T(4,128)} %start_hbm.1), custom_call_target="tpu_custom_call" | custom-call | flops 1000000 | bytes 500000 | tf_op jit(solution)/shard_map/pallas_call | solution.py:342
  2.4 0.0 copy-start.2
  2.4 14.8 %all-to-all-start = ((f32[64,5,128]{2,1,0:T(8,128)}), f32[64,5,128]{2,1,0:T(8,128)S(1)}, u32[]{:S(2)}, u32[]{:S(2)}) async-start(f32[64,5,128]{2,1,0:T(8,128)} %shard_map.77), calls=%async_computation | async-start | bytes 524288 | tf_op jit(solution)/shard_map/all_to_all | solution.py:354
  17.3 0.9 %shard_map.79 = (bf16[2,256,256]{2,1,0:T(8,128)(2,1)S(1)}, bf16[2,256,256]{2,1,0:T(8,128)(2,1)S(1)}, bf16[2,128,256]{2,1,0:T(8,128)(2,1)S(1)}, f32[2,4,64,128]{3,2,1,0:T(8,128)S(1)}) custom-call(f32[4,64,64]{2,1,0:T(8,128)S(1)} %copy-done.2, f32[4,2,64,64]{3,2,1,0:T(8,128)S(1)} %copy-done.1, f32[4,4,64,64]{3,2,1,0:T(8,128)S(1)} %copy-done), custom_call_target="tpu_custom_call" | custom-call | flops 4000000000 | bytes 500000 | tf_op jit(solution)/shard_map/pallas_call | solution.py:356
  18.1 12.5 %all-to-all-done.in_ref = f32[64,5,128]{2,1,0:T(8,128)S(1)} async-done(((f32[64,5,128]{2,1,0:T(8,128)}), f32[64,5,128]{2,1,0:T(8,128)S(1)}, u32[]{:S(2)}, u32[]{:S(2)}) %all-to-all-start) | async-done | bytes 163872 | tf_op jit(solution)/shard_map/all_to_all | solution.py:354
  30.6 0.1 shard_map.78
  30.8 1.5 %collective-permute-start.3 = (f32[128,128]{1,0:T(8,128)S(1)}, f32[128,128]{1,0:T(8,128)S(1)}, u32[]{:S(2)}, u32[]{:S(2)}) collective-permute-start(f32[128,128]{1,0:T(8,128)S(1)} %get-tuple-element.14.after_ref.start_ref), channel_id=1, source_target_pairs={{0,2},{8,0},{16,8},{24,16},{26,24},{18,26},{10,18},{2,10},{1,3},{9... | collective-permute-start | bytes 196616 | tf_op jit(solution)/shard_map/ppermute | solution.py:327
  32.3 0.5 collective-permute-start.2
  32.8 0.7 collective-permute-start.1
  33.5 1.3 %collective-permute-start = (f32[128,128]{1,0:T(8,128)S(1)}, f32[128,128]{1,0:T(8,128)S(1)}, u32[]{:S(2)}, u32[]{:S(2)}) collective-permute-start(f32[128,128]{1,0:T(8,128)S(1)} %get-tuple-element.14.after_ref.start_ref), channel_id=1, source_target_pairs={{0,32},{32,64},{64,96},{96,97},{97,65},{65,33},{33,1},{1,0},{2,34}... | collective-permute-start | bytes 196616 | tf_op jit(solution)/shard_map/ppermute | solution.py:327
  34.9 2.0 %shard_map.80.map_ref = f32[32,64,128]{2,1,0:T(8,128)S(1)} custom-call(f32[128,128]{1,0:T(8,128)S(1)} %get-tuple-element.20.kind_ref, bf16[128,128]{1,0:T(8,128)(2,1)S(1)} %get-tuple-element.15.mask_a_ref, bf16[128,128]{1,0:T(8,128)(2,1)S(1)} %get-tuple-element.16.mask_b_ref, bf16[2,256,256]{2,1,0:T(8,128)(2,1)S(1)} %get-tuple-element.17.tables_ref, ...), custom_call_target="tpu_custom_call" | custom-call | flops 4000000000 | bytes 500000 | tf_op jit(solution)/shard_map/pallas_call | solution.py:366
  36.9 0.2 collective-permute-done.1.n1_ref
  37.1 0.7 collective-permute-done.n0_ref
  37.8 3.3 %shard_map.81 = (f32[128,128]{1,0:T(8,128)S(1)}, f32[256,128]{1,0:T(8,128)S(1)}) custom-call(f32[128,128]{1,0:T(8,128)S(1)} %get-tuple-element.13.rhs_ref, f32[128,128]{1,0:T(8,128)S(1)} %get-tuple-element.14.after_ref.start_ref, f32[128,128]{1,0:T(8,128)S(1)} %collective-permute-done.n0_ref, f32[128,128]{1,0:T(8,128)S(1)} %collective-permute-done.1.n1_ref, ...), custom_call_target="tpu_custom_call" | custom-call | flops 4000000000 | bytes 500000 | tf_op jit(solution)/shard_map/pallas_call | solution.py:380
  41.1 1.5 %collective-permute-start.7 = (f32[128,128]{1,0:T(8,128)S(1)}, f32[128,128]{1,0:T(8,128)S(1)}, u32[]{:S(2)}, u32[]{:S(2)}) collective-permute-start(f32[128,128]{1,0:T(8,128)S(1)} %get-tuple-element.22.after_ref.forward_ref), channel_id=1, source_target_pairs={{0,2},{8,0},{16,8},{24,16},{26,24},{18,26},{10,18},{2,10},{1,3},{9... | collective-permute-start | bytes 196616 | tf_op jit(solution)/shard_map/ppermute | solution.py:327
  42.6 0.5 collective-permute-start.6
  43.1 1.3 %collective-permute-start.5 = (f32[128,128]{1,0:T(8,128)S(1)}, f32[128,128]{1,0:T(8,128)S(1)}, u32[]{:S(2)}, u32[]{:S(2)}) collective-permute-start(f32[128,128]{1,0:T(8,128)S(1)} %get-tuple-element.22.after_ref.forward_ref), channel_id=1, source_target_pairs={{0,1},{32,0},{64,32},{96,64},{97,96},{65,97},{33,65},{1,33},{2,3},... | collective-permute-start | bytes 196616 | tf_op jit(solution)/shard_map/ppermute | solution.py:327
  44.5 0.7 collective-permute-start.4
  45.1 2.0 %shard_map.82.map_ref = f32[32,64,128]{2,1,0:T(8,128)S(1)} custom-call(f32[128,128]{1,0:T(8,128)S(1)} %get-tuple-element.20.kind_ref, bf16[128,128]{1,0:T(8,128)(2,1)S(1)} %get-tuple-element.15.mask_a_ref, bf16[128,128]{1,0:T(8,128)(2,1)S(1)} %get-tuple-element.16.mask_b_ref, bf16[2,256,256]{2,1,0:T(8,128)(2,1)S(1)} %get-tuple-element.17.tables_ref, ...), custom_call_target="tpu_custom_call" | custom-call | flops 4000000000 | bytes 500000 | tf_op jit(solution)/shard_map/pallas_call | solution.py:366
  47.1 0.3 collective-permute-done.5.n1_ref
  47.4 1.3 %collective-permute-done.4.n0_ref = f32[128,128]{1,0:T(8,128)S(1)} collective-permute-done((f32[128,128]{1,0:T(8,128)S(1)}, f32[128,128]{1,0:T(8,128)S(1)}, u32[]{:S(2)}, u32[]{:S(2)}) %collective-permute-start.4) | collective-permute-done | bytes 65568 | tf_op jit(solution)/shard_map/ppermute | solution.py:327
  48.7 3.3 %shard_map.83 = f32[64,4,128]{2,1,0:T(4,128)S(1)} custom-call(f32[128,128]{1,0:T(8,128)S(1)} %get-tuple-element.22.after_ref.forward_ref, f32[256,128]{1,0:T(8,128)S(1)} %get-tuple-element.23.given_ref, f32[128,128]{1,0:T(8,128)S(1)} %collective-permute-done.4.n0_ref, f32[128,128]{1,0:T(8,128)S(1)} %collective-permute-done.5.n1_ref, ...), custom_call_target="tpu_custom_call" | custom-call | flops 4000000000 | bytes 500000 | tf_op jit(solution)/shard_map/pallas_call | solution.py:390
  52.0 18.2 %all_to_all.10.in_ref = f32[64,4,128]{2,1,0:T(4,128)S(1)} all-to-all(f32[64,4,128]{2,1,0:T(4,128)S(1)} %shard_map.83), channel_id=1, replica_groups=mesh['ah'=2,'am'=2,'al'=2,'b'=4,'c'=2,'gx'=2,'gy'=2] {'ah','am','al','b'..., dimensions={0} | all-to-all | bytes 262144 | tf_op jit(solution)/shard_map/all_to_all | solution.py:397
  70.2 0.7 %shard_map.84 = (f32[2,4,4,512]{3,2,1,0:T(4,128)}, f32[2,4,4,512]{3,2,1,0:T(4,128)}) custom-call(f32[64,4,128]{2,1,0:T(4,128)S(1)} %all_to_all.10.in_ref), custom_call_target="tpu_custom_call" | custom-call | flops 1000000 | bytes 500000 | tf_op jit(solution)/shard_map/pallas_call | solution.py:399
  (9 shorter events, 0.0 us)
Async XLA Ops:
  0.6 16.6 %copy-start = (f32[4,4,64,64]{3,2,1,0:T(8,128)S(1)}, f32[4,4,64,64]{3,2,1,0:T(8,128)}, u32[]{:S(2)}) copy-start(f32[4,4,64,64]{3,2,1,0:T(8,128)} %side_ref.1) | copy-start | bytes 786436
  2.4 14.8 %copy-start.1 = (f32[4,2,64,64]{3,2,1,0:T(8,128)S(1)}, f32[4,2,64,64]{3,2,1,0:T(8,128)}, u32[]{:S(2)}) copy-start(f32[4,2,64,64]{3,2,1,0:T(8,128)} %z_ref.1) | copy-start | bytes 393220
  2.4 14.8 %copy-start.2 = (f32[4,64,64]{2,1,0:T(8,128)S(1)}, f32[4,64,64]{2,1,0:T(8,128)}, u32[]{:S(2)}) copy-start(f32[4,64,64]{2,1,0:T(8,128)} %diag_ref.1) | copy-start | bytes 196612
  2.4 28.2 %all-to-all-start = ((f32[64,5,128]{2,1,0:T(8,128)}), f32[64,5,128]{2,1,0:T(8,128)S(1)}, u32[]{:S(2)}, u32[]{:S(2)}) async-start(f32[64,5,128]{2,1,0:T(8,128)} %shard_map.77), calls=%async_computation | async-start | bytes 524288 | tf_op jit(solution)/shard_map/all_to_all | solution.py:354
  30.8 6.1 %collective-permute-start.3 = (f32[128,128]{1,0:T(8,128)S(1)}, f32[128,128]{1,0:T(8,128)S(1)}, u32[]{:S(2)}, u32[]{:S(2)}) collective-permute-start(f32[128,128]{1,0:T(8,128)S(1)} %get-tuple-element.14.after_ref.start_ref), channel_id=1, source_target_pairs={{0,2},{8,0},{16,8},{24,16},{26,24},{18,26},{10,18},{2,10},{1,3},{9... | collective-permute-start | bytes 196616 | tf_op jit(solution)/shard_map/ppermute | solution.py:327
  32.3 4.6 %collective-permute-start.2 = (f32[128,128]{1,0:T(8,128)S(1)}, f32[128,128]{1,0:T(8,128)S(1)}, u32[]{:S(2)}, u32[]{:S(2)}) collective-permute-start(f32[128,128]{1,0:T(8,128)S(1)} %get-tuple-element.14.after_ref.start_ref), channel_id=1, source_target_pairs={{0,8},{8,16},{16,24},{24,26},{26,18},{18,10},{10,2},{2,0},{1,9},{9... | collective-permute-start | bytes 196616 | tf_op jit(solution)/shard_map/ppermute | solution.py:327
  32.8 4.3 %collective-permute-start.1 = (f32[128,128]{1,0:T(8,128)S(1)}, f32[128,128]{1,0:T(8,128)S(1)}, u32[]{:S(2)}, u32[]{:S(2)}) collective-permute-start(f32[128,128]{1,0:T(8,128)S(1)} %get-tuple-element.14.after_ref.start_ref), channel_id=1, source_target_pairs={{0,1},{32,0},{64,32},{96,64},{97,96},{65,97},{33,65},{1,33},{2,3},... | collective-permute-start | bytes 196616 | tf_op jit(solution)/shard_map/ppermute | solution.py:327
  33.5 4.3 %collective-permute-start = (f32[128,128]{1,0:T(8,128)S(1)}, f32[128,128]{1,0:T(8,128)S(1)}, u32[]{:S(2)}, u32[]{:S(2)}) collective-permute-start(f32[128,128]{1,0:T(8,128)S(1)} %get-tuple-element.14.after_ref.start_ref), channel_id=1, source_target_pairs={{0,32},{32,64},{64,96},{96,97},{97,65},{65,33},{33,1},{1,0},{2,34}... | collective-permute-start | bytes 196616 | tf_op jit(solution)/shard_map/ppermute | solution.py:327
  41.1 6.0 %collective-permute-start.7 = (f32[128,128]{1,0:T(8,128)S(1)}, f32[128,128]{1,0:T(8,128)S(1)}, u32[]{:S(2)}, u32[]{:S(2)}) collective-permute-start(f32[128,128]{1,0:T(8,128)S(1)} %get-tuple-element.22.after_ref.forward_ref), channel_id=1, source_target_pairs={{0,2},{8,0},{16,8},{24,16},{26,24},{18,26},{10,18},{2,10},{1,3},{9... | collective-permute-start | bytes 196616 | tf_op jit(solution)/shard_map/ppermute | solution.py:327
  42.6 4.5 %collective-permute-start.6 = (f32[128,128]{1,0:T(8,128)S(1)}, f32[128,128]{1,0:T(8,128)S(1)}, u32[]{:S(2)}, u32[]{:S(2)}) collective-permute-start(f32[128,128]{1,0:T(8,128)S(1)} %get-tuple-element.22.after_ref.forward_ref), channel_id=1, source_target_pairs={{0,8},{8,16},{16,24},{24,26},{26,18},{18,10},{10,2},{2,0},{1,9},{9... | collective-permute-start | bytes 196616 | tf_op jit(solution)/shard_map/ppermute | solution.py:327
  43.1 4.3 %collective-permute-start.5 = (f32[128,128]{1,0:T(8,128)S(1)}, f32[128,128]{1,0:T(8,128)S(1)}, u32[]{:S(2)}, u32[]{:S(2)}) collective-permute-start(f32[128,128]{1,0:T(8,128)S(1)} %get-tuple-element.22.after_ref.forward_ref), channel_id=1, source_target_pairs={{0,1},{32,0},{64,32},{96,64},{97,96},{65,97},{33,65},{1,33},{2,3},... | collective-permute-start | bytes 196616 | tf_op jit(solution)/shard_map/ppermute | solution.py:327
  44.5 4.3 %collective-permute-start.4 = (f32[128,128]{1,0:T(8,128)S(1)}, f32[128,128]{1,0:T(8,128)S(1)}, u32[]{:S(2)}, u32[]{:S(2)}) collective-permute-start(f32[128,128]{1,0:T(8,128)S(1)} %get-tuple-element.22.after_ref.forward_ref), channel_id=1, source_target_pairs={{0,32},{32,64},{64,96},{96,97},{97,65},{65,33},{33,1},{1,0},{2,34}... | collective-permute-start | bytes 196616 | tf_op jit(solution)/shard_map/ppermute | solution.py:327

commit v4 on v3

--- a/solution.py
+++ b/solution.py
@@ -61,24 +61,7 @@
     return lax.axis_index("gx") * 3, lax.axis_index("gy") * 3
 
 
-def pack(mat_ref, rhs_ref, start_ref, out_ref):
-    flip_x, flip_y = flips()
-    low = lax.broadcasted_iota(jnp.int32, (1, LANES), 1) < DOFS
-    for y in range(4):
-        for x in range(4):
-            block = block_of(y, x, flip_y, flip_x)
-            kinds = jnp.where(low, mat_ref[0, y, x].astype(F32), mat_ref[1, y, x].astype(F32))
-            for part in range(4):
-                out_ref[block + (part // 2) * 32 + part % 2, 4:5, :] = kinds
-            for p in range(2):
-                for part in range(4):
-                    lanes = slice(part * LANES, (part + 1) * LANES)
-                    slot = block + (part // 2) * 32 + part % 2
-                    out_ref[slot, p : p + 1, :] = rhs_ref[p, y, x : x + 1, lanes]
-                    out_ref[slot, 2 + p : 3 + p, :] = start_ref[p, y, x : x + 1, lanes]
-
-
-def pack_kernel(mat_hbm, rhs_hbm, start_hbm, out_ref, mat_ref, rhs_ref, start_ref, sems):
+def pack_kernel(mat_hbm, rhs_hbm, start_hbm, out_hbm, mat_ref, rhs_ref, start_ref, out_ref, sems, out_sems):
     copies = [
         pltpu.make_async_copy(source, target, sems.at[k])
         for k, (source, target) in enumerate(((mat_hbm, mat_ref), (rhs_hbm, rhs_ref), (start_hbm, start_ref)))
@@ -87,20 +70,46 @@
         copy.start()
     for copy in copies:
         copy.wait()
-    pack(mat_ref, rhs_ref, start_ref, out_ref)
-
-
-def unpack_kernel(in_ref, forward_ref, backward_ref):
     flip_x, flip_y = flips()
+    low = lax.broadcasted_iota(jnp.int32, (1, LANES), 1) < DOFS
+    leaving = []
     for y in range(4):
         for x in range(4):
             block = block_of(y, x, flip_y, flip_x)
+            kinds = jnp.where(low, mat_ref[0, y, x].astype(F32), mat_ref[1, y, x].astype(F32))
             for part in range(4):
                 lanes = slice(part * LANES, (part + 1) * LANES)
                 slot = block + (part // 2) * 32 + part % 2
+                out_ref[slot, 4:5, :] = kinds
                 for p in range(2):
-                    forward_ref[p, y, x : x + 1, lanes] = in_ref[slot, p : p + 1, :]
-                    backward_ref[p, y, x : x + 1, lanes] = in_ref[slot, 2 + p : 3 + p, :]
+                    out_ref[slot, p : p + 1, :] = rhs_ref[p, y, x : x + 1, lanes]
+                    out_ref[slot, 2 + p : 3 + p, :] = start_ref[p, y, x : x + 1, lanes]
+        for half in range(2):
+            slots = pl.ds(half * 32 + (y ^ flip_y) * 8, 8)
+            copy = pltpu.make_async_copy(out_ref.at[slots], out_hbm.at[slots], out_sems.at[y, half])
+            copy.start()
+            leaving.append(copy)
+    for copy in leaving:
+        copy.wait()
+
+
+def unpack_kernel(in_ref, forward_hbm, backward_hbm, forward_ref, backward_ref, sems):
+    flip_x, flip_y = flips()
+    leaving = []
+    for k, (field_ref, field_hbm) in enumerate(((forward_ref, forward_hbm), (backward_ref, backward_hbm))):
+        for p in range(2):
+            for y in range(4):
+                for x in range(4):
+                    block = block_of(y, x, flip_y, flip_x)
+                    for part in range(4):
+                        lanes = slice(part * LANES, (part + 1) * LANES)
+                        slot = block + (part // 2) * 32 + part % 2
+                        field_ref[p, y, x : x + 1, lanes] = in_ref[slot, 2 * k + p : 2 * k + p + 1, :]
+            copy = pltpu.make_async_copy(field_ref.at[p], field_hbm.at[p], sems.at[k, p])
+            copy.start()
+            leaving.append(copy)
+    for copy in leaving:
+        copy.wait()
 
 
 def masks_of(kind):
@@ -193,21 +202,23 @@
     return jnp.where(low, state[:CHUNKS], state[CHUNKS:])
 
 
-def chain(const_ref, mask_a_ref, mask_b_ref, table_ref, map_ref, ends_ref, heads_ref, out_ref, descending):
+def rows_of(step):
+    return pl.ds(step * CHUNKS, CHUNKS)
+
+
+def chain(known, mask_a_ref, mask_b_ref, table_ref, map_ref, ends_ref, heads_ref, out_ref, descending):
     steps, chunks = chain_order(descending)
-
-    def known(step):
-        rows = pl.ds(step * CHUNKS, CHUNKS)
-        return jnp.concatenate([const_ref[rows, :], const_ref[pl.ds(ROWS + step * CHUNKS, CHUNKS), :]], axis=0)
+    consts = {}
 
     def advance(state, step):
-        rows = pl.ds(step * CHUNKS, CHUNKS)
+        rows = rows_of(step)
         wide = widened(state, both(mask_a_ref[rows, :]), both(mask_b_ref[rows, :]))
         product = jnp.dot(wide, table_ref[...], preferred_element_type=F32)
-        return known(step) - fold(product)
-
-    state = known(steps[0])
+        return consts[step] - fold(product)
+
+    state = consts[steps[0]] = known(steps[0])
     for step in steps[1:]:
+        consts[step] = known(step)
         state = advance(state, step)
     ends_ref[...] = pairs_of(state)
 
@@ -234,12 +245,11 @@
         out_ref[pl.ds(step * CHUNKS, CHUNKS), :] = pairs_of(state)
 
 
-def beside_inside(refs):
+def inside():
     x, y = lax.axis_index("b"), lax.axis_index("am") * 2 + lax.axis_index("al")
     x = jnp.where(lax.axis_index("gx") == 1, 7 - x, x)
     y = jnp.where(lax.axis_index("gy") == 1, 7 - y, y)
-    inside = (y > 0, y < 7, x > 0, x < 7)
-    return [jnp.where(here, ref[...], 0.0) for here, ref in zip(inside, refs)]
+    return y > 0, y < 7, x > 0, x < 7
 
 
 def stacked(value):
@@ -275,25 +285,41 @@
     return jnp.dot(stacked(doubled(piece)), pair_ref[...], preferred_element_type=F32)
 
 
+def side_known(step, here, refs, sides_ref):
+    rows = rows_of(step)
+    return side_product([jnp.where(ok, ref[rows, :], 0.0) for ok, ref in zip(here, refs)], sides_ref)
+
+
 def forward_kernel(rhs_ref, start_ref, n0_ref, n1_ref, n2_ref, n3_ref, mask_a_ref, mask_b_ref, tables_ref,
-                   sides_ref, own_ref, map_ref, forward_ref, given_ref, const_ref, ends_ref, heads_ref):
-    mask_a, mask_b = both(mask_a_ref[...].astype(F32)), both(mask_b_ref[...].astype(F32))
-    start = start_ref[...]
-    following = jnp.concatenate([start[1:CHUNKS], jnp.zeros((1, LANES), F32)], axis=0)
-    upper = jnp.concatenate([start[CHUNKS:], following], axis=0)
-    product = side_product(beside_inside((n0_ref, n1_ref, n2_ref, n3_ref)), sides_ref)
-    given = chosen(product + own_product(upper, own_ref.at[0]), mask_a, mask_b)
-    given_ref[...] = given
-    const_ref[...] = chosen(own_product(rhs_ref[...], own_ref.at[1]), mask_a, mask_b) - given
-    chain(const_ref, mask_a_ref, mask_b_ref, tables_ref.at[0], map_ref, ends_ref, heads_ref, forward_ref, False)
+                   sides_ref, own_ref, map_ref, forward_ref, given_ref, ends_ref, heads_ref):
+    here = inside()
+
+    def known(step):
+        rows = rows_of(step)
+        if step + 1 < STEPS:
+            upper = start_ref[rows_of(step + 1), :]
+        else:
+            upper = jnp.concatenate([start_ref[1:CHUNKS, :], jnp.zeros((1, LANES), F32)], axis=0)
+        mask_a, mask_b = both(mask_a_ref[rows, :].astype(F32)), both(mask_b_ref[rows, :].astype(F32))
+        product = side_known(step, here, (n0_ref, n1_ref, n2_ref, n3_ref), sides_ref)
+        given = chosen(product + own_product(upper, own_ref.at[0]), mask_a, mask_b)
+        given_ref[step] = given
+        return chosen(own_product(rhs_ref[rows, :], own_ref.at[1]), mask_a, mask_b) - given
+
+    chain(known, mask_a_ref, mask_b_ref, tables_ref.at[0], map_ref, ends_ref, heads_ref, forward_ref, False)
 
 
 def backward_kernel(forward_ref, given_ref, n0_ref, n1_ref, n2_ref, n3_ref, mask_a_ref, mask_b_ref, tables_ref,
-                    sides_ref, map_ref, out_ref, const_ref, ends_ref, heads_ref, backward_ref):
-    mask_a, mask_b = both(mask_a_ref[...].astype(F32)), both(mask_b_ref[...].astype(F32))
-    terms = chosen(side_product(beside_inside((n0_ref, n1_ref, n2_ref, n3_ref)), sides_ref), mask_a, mask_b)
-    const_ref[...] = doubled(forward_ref[...]) + (given_ref[...] - terms)
-    chain(const_ref, mask_a_ref, mask_b_ref, tables_ref.at[1], map_ref, ends_ref, heads_ref, backward_ref, True)
+                    sides_ref, map_ref, out_ref, ends_ref, heads_ref, backward_ref):
+    here = inside()
+
+    def known(step):
+        rows = rows_of(step)
+        mask_a, mask_b = both(mask_a_ref[rows, :].astype(F32)), both(mask_b_ref[rows, :].astype(F32))
+        terms = chosen(side_known(step, here, (n0_ref, n1_ref, n2_ref, n3_ref), sides_ref), mask_a, mask_b)
+        return doubled(forward_ref[rows, :]) + (given_ref[step] - terms)
+
+    chain(known, mask_a_ref, mask_b_ref, tables_ref.at[1], map_ref, ends_ref, heads_ref, backward_ref, True)
     for step in range(STEPS):
         for chunk in range(CHUNKS):
             block, p = chunk * (STEPS // 2) + step // 2, step % 2
@@ -306,12 +332,12 @@
     return jax.ShapeDtypeStruct(dims, dtype)
 
 
-def call(kernel, outs, ins, scratch=(), flops=1000000, limit=16 * 1024 * 1024):
+def call(kernel, outs, ins, scratch=(), flops=1000000, limit=16 * 1024 * 1024, to=VMEM):
     return pl.pallas_call(
         kernel,
         out_shape=outs,
         in_specs=ins,
-        out_specs=jax.tree.map(lambda _: VMEM, outs),
+        out_specs=jax.tree.map(lambda _: to, outs),
         scratch_shapes=scratch,
         cost_estimate=pl.CostEstimate(flops=flops, bytes_accessed=500000, transcendentals=0),
         compiler_params=pltpu.CompilerParams(vmem_limit_bytes=limit),
@@ -347,9 +373,12 @@
             pltpu.SMEM(material.shape, jnp.int32),
             pltpu.VMEM(rhs_field.shape, F32),
             pltpu.VMEM(rhs_field.shape, F32),
+            pltpu.VMEM((PEERS, SLOTS, LANES), F32),
             pltpu.SemaphoreType.DMA((3,)),
+            pltpu.SemaphoreType.DMA((4, 2)),
         ],
         limit=None,
+        to=HBM,
     )(material, rhs_field, start_field)
     arrived = lax.all_to_all(packed, GZ, 0, 0, tiled=True)
     square = shape(2, 256, 256, dtype=BF16)
@@ -373,13 +402,12 @@
 
     map_f = maps(0, start)
     chain_scratch = [
-        pltpu.VMEM((2 * ROWS, LANES), F32),
         pltpu.VMEM((CHUNKS, LANES), F32),
         pltpu.VMEM((CHUNKS, LANES), F32),
     ]
     forward, given = call(
         forward_kernel,
-        (field, shape(2 * ROWS, LANES)),
+        (field, shape(STEPS, 2 * CHUNKS, LANES)),
         [VMEM] * 12,
         chain_scratch,
         flops=4000000000,
@@ -396,7 +424,17 @@
     )(forward, given, *beside, mask_a, mask_b, tables, sides, map_b)
     returned = lax.all_to_all(ready, GZ, 0, 0, tiled=True)
     cells = shape(*rhs_field.shape)
-    return call(unpack_kernel, (cells, cells), [VMEM])(returned)
+    return call(
+        unpack_kernel,
+        (cells, cells),
+        [VMEM],
+        [
+            pltpu.VMEM(rhs_field.shape, F32),
+            pltpu.VMEM(rhs_field.shape, F32),
+            pltpu.SemaphoreType.DMA((2, 2)),
+        ],
+        to=HBM,
+    )(returned)
 
 
 def solution(mesh):

time: 71.1 us -> 70.8 us (level)
  no operation moved by 1% of the time
where the time goes in v4:
time: 70.8 us; the launch traced here: 70.6 us
  starting transfers between devices  22.9 us (32%)
  blocking collectives  18.2 us (26%)
  waiting for transfers between devices  15 us (21%)
  Pallas kernels  13.6 us (19%)
  between operations  0.78 us (1%)
    all_to_all x1, blocking collectives, per_device(): returned = lax.all_to_all(ready, GZ, 0, 0, tiled=True)  18.2 us
    all_to_all x1, starting transfers between devices, per_device(): arrived = lax.all_to_all(packed, GZ, 0, 0, tiled=True)  14.8 us
    all_to_all x1, waiting for transfers between devices, per_device(): arrived = lax.all_to_all(packed, GZ, 0, 0, tiled=True)  12.5 us
    ppermute x8, starting transfers between devices, moved(): return lax.ppermute(value, axes, pairs)  8.13 us
    pallas_call x2, Pallas kernels, maps(): call(functools.partial(maps_kernel, q), shape(CHUNKS, DOFS, LANES), [VMEM...  3.98 us
    pallas_call x1, Pallas kernels, per_device(): call(forward_kernel, (field, shape(STEPS, 2 * CHUNKS, LANES)), [VMEM] * 1...  3.07 us
    pallas_call x1, Pallas kernels, per_device(): call(backward_kernel, shape(PEERS, 4, LANES), [VMEM] * 11, chain_scratch...  3.07 us
    ppermute x8, waiting for transfers between devices, moved(): return lax.ppermute(value, axes, pairs)  2.48 us
  transfers between devices with their start and end apart: 9, of which 5 were waited for; matrix products, arithmetic and copies ran while one was open for 0% of the time, Pallas kernels for 7%

profile of v4, /device:TPU:2, one launch (start us, length us, event | category | flops | bytes accessed | tf_op | source)
XLA Modules:
  0.0 70.6 jit_solution(10685740228522543281)
XLA Ops:
  0.6 1.8 %shard_map.77 = f32[64,5,128]{2,1,0:T(8,128)} custom-call(s32[2,4,4]{2,1,0:T(4,128)} %mat_hbm.1, f32[2,4,4,512]{3,2,1,0:T(4,128)} %rhs_hbm.1, f32[2,4,4,512]{3,2,1,0:T(4,128)} %start_hbm.1), custom_call_target="tpu_custom_call" | custom-call | flops 1000000 | bytes 500000 | tf_op jit(solution)/shard_map/pallas_call | solution.py:368
  2.4 0.0 copy-start.2
  2.4 14.8 %all-to-all-start = ((f32[64,5,128]{2,1,0:T(8,128)}), f32[64,5,128]{2,1,0:T(8,128)S(1)}, u32[]{:S(2)}, u32[]{:S(2)}) async-start(f32[64,5,128]{2,1,0:T(8,128)} %shard_map.77), calls=%async_computation | async-start | bytes 524288 | tf_op jit(solution)/shard_map/all_to_all | solution.py:383
  17.3 0.9 %shard_map.79 = (bf16[2,256,256]{2,1,0:T(8,128)(2,1)S(1)}, bf16[2,256,256]{2,1,0:T(8,128)(2,1)S(1)}, bf16[2,128,256]{2,1,0:T(8,128)(2,1)S(1)}, f32[2,4,64,128]{3,2,1,0:T(8,128)S(1)}) custom-call(f32[4,64,64]{2,1,0:T(8,128)S(1)} %copy-done.2, f32[4,2,64,64]{3,2,1,0:T(8,128)S(1)} %copy-done.1, f32[4,4,64,64]{3,2,1,0:T(8,128)S(1)} %copy-done), custom_call_target="tpu_custom_call" | custom-call | flops 4000000000 | bytes 500000 | tf_op jit(solution)/shard_map/pallas_call | solution.py:385
  18.1 12.5 %all-to-all-done.in_ref = f32[64,5,128]{2,1,0:T(8,128)S(1)} async-done(((f32[64,5,128]{2,1,0:T(8,128)}), f32[64,5,128]{2,1,0:T(8,128)S(1)}, u32[]{:S(2)}, u32[]{:S(2)}) %all-to-all-start) | async-done | bytes 163872 | tf_op jit(solution)/shard_map/all_to_all | solution.py:383
  30.6 0.1 shard_map.78
  30.8 1.5 %collective-permute-start.3 = (f32[128,128]{1,0:T(8,128)S(1)}, f32[128,128]{1,0:T(8,128)S(1)}, u32[]{:S(2)}, u32[]{:S(2)}) collective-permute-start(f32[128,128]{1,0:T(8,128)S(1)} %get-tuple-element.14.after_ref.start_ref), channel_id=1, source_target_pairs={{0,2},{8,0},{16,8},{24,16},{26,24},{18,26},{10,18},{2,10},{1,3},{9... | collective-permute-start | bytes 196616 | tf_op jit(solution)/shard_map/ppermute | solution.py:353
  32.3 0.5 collective-permute-start.2
  32.8 0.7 collective-permute-start.1
  33.5 1.4 %collective-permute-start = (f32[128,128]{1,0:T(8,128)S(1)}, f32[128,128]{1,0:T(8,128)S(1)}, u32[]{:S(2)}, u32[]{:S(2)}) collective-permute-start(f32[128,128]{1,0:T(8,128)S(1)} %get-tuple-element.14.after_ref.start_ref), channel_id=1, source_target_pairs={{0,32},{32,64},{64,96},{96,97},{97,65},{65,33},{33,1},{1,0},{2,34}... | collective-permute-start | bytes 196616 | tf_op jit(solution)/shard_map/ppermute | solution.py:353
  34.9 2.0 %shard_map.80.map_ref = f32[32,64,128]{2,1,0:T(8,128)S(1)} custom-call(f32[128,128]{1,0:T(8,128)S(1)} %get-tuple-element.20.kind_ref, bf16[128,128]{1,0:T(8,128)(2,1)S(1)} %get-tuple-element.15.mask_a_ref, bf16[128,128]{1,0:T(8,128)(2,1)S(1)} %get-tuple-element.16.mask_b_ref, bf16[2,256,256]{2,1,0:T(8,128)(2,1)S(1)} %get-tuple-element.17.tables_ref, ...), custom_call_target="tpu_custom_call" | custom-call | flops 4000000000 | bytes 500000 | tf_op jit(solution)/shard_map/pallas_call | solution.py:395
  36.9 0.2 collective-permute-done.1.n1_ref
  37.1 0.7 collective-permute-done.n0_ref
  37.8 3.1 %shard_map.81 = (f32[128,128]{1,0:T(8,128)S(1)}, f32[4,64,128]{2,1,0:T(8,128)S(1)}) custom-call(f32[128,128]{1,0:T(8,128)S(1)} %get-tuple-element.13.rhs_ref, f32[128,128]{1,0:T(8,128)S(1)} %get-tuple-element.14.after_ref.start_ref, f32[128,128]{1,0:T(8,128)S(1)} %collective-permute-done.n0_ref, f32[128,128]{1,0:T(8,128)S(1)} %collective-permute-done.1.n1_ref, ...), custom_call_target="tpu_custom_call" | custom-call | flops 4000000000 | bytes 500000 | tf_op jit(solution)/shard_map/pallas_call | solution.py:408
  40.9 1.5 %collective-permute-start.7 = (f32[128,128]{1,0:T(8,128)S(1)}, f32[128,128]{1,0:T(8,128)S(1)}, u32[]{:S(2)}, u32[]{:S(2)}) collective-permute-start(f32[128,128]{1,0:T(8,128)S(1)} %get-tuple-element.22.after_ref.forward_ref), channel_id=1, source_target_pairs={{0,2},{8,0},{16,8},{24,16},{26,24},{18,26},{10,18},{2,10},{1,3},{9... | collective-permute-start | bytes 196616 | tf_op jit(solution)/shard_map/ppermute | solution.py:353
  42.4 0.5 collective-permute-start.6
  42.9 1.3 %collective-permute-start.5 = (f32[128,128]{1,0:T(8,128)S(1)}, f32[128,128]{1,0:T(8,128)S(1)}, u32[]{:S(2)}, u32[]{:S(2)}) collective-permute-start(f32[128,128]{1,0:T(8,128)S(1)} %get-tuple-element.22.after_ref.forward_ref), channel_id=1, source_target_pairs={{0,1},{32,0},{64,32},{96,64},{97,96},{65,97},{33,65},{1,33},{2,3},... | collective-permute-start | bytes 196616 | tf_op jit(solution)/shard_map/ppermute | solution.py:353
  44.3 0.7 collective-permute-start.4
  44.9 2.0 %shard_map.82.map_ref = f32[32,64,128]{2,1,0:T(8,128)S(1)} custom-call(f32[128,128]{1,0:T(8,128)S(1)} %get-tuple-element.20.kind_ref, bf16[128,128]{1,0:T(8,128)(2,1)S(1)} %get-tuple-element.15.mask_a_ref, bf16[128,128]{1,0:T(8,128)(2,1)S(1)} %get-tuple-element.16.mask_b_ref, bf16[2,256,256]{2,1,0:T(8,128)(2,1)S(1)} %get-tuple-element.17.tables_ref, ...), custom_call_target="tpu_custom_call" | custom-call | flops 4000000000 | bytes 500000 | tf_op jit(solution)/shard_map/pallas_call | solution.py:395
  46.9 0.3 collective-permute-done.5.n1_ref
  47.2 1.3 %collective-permute-done.4.n0_ref = f32[128,128]{1,0:T(8,128)S(1)} collective-permute-done((f32[128,128]{1,0:T(8,128)S(1)}, f32[128,128]{1,0:T(8,128)S(1)}, u32[]{:S(2)}, u32[]{:S(2)}) %collective-permute-start.4) | collective-permute-done | bytes 65568 | tf_op jit(solution)/shard_map/ppermute | solution.py:353
  48.5 3.1 %shard_map.83 = f32[64,4,128]{2,1,0:T(4,128)S(1)} custom-call(f32[128,128]{1,0:T(8,128)S(1)} %get-tuple-element.22.after_ref.forward_ref, f32[4,64,128]{2,1,0:T(8,128)S(1)} %get-tuple-element.23.given_ref, f32[128,128]{1,0:T(8,128)S(1)} %collective-permute-done.4.n0_ref, f32[128,128]{1,0:T(8,128)S(1)} %collective-permute-done.5.n1_ref, ...), custom_call_target="tpu_custom_call" | custom-call | flops 4000000000 | bytes 500000 | tf_op jit(solution)/shard_map/pallas_call | solution.py:418
  51.6 18.2 %all_to_all.10.in_ref = f32[64,4,128]{2,1,0:T(4,128)S(1)} all-to-all(f32[64,4,128]{2,1,0:T(4,128)S(1)} %shard_map.83), channel_id=1, replica_groups=mesh['ah'=2,'am'=2,'al'=2,'b'=4,'c'=2,'gx'=2,'gy'=2] {'ah','am','al','b'..., dimensions={0} | all-to-all | bytes 262144 | tf_op jit(solution)/shard_map/all_to_all | solution.py:425
  69.8 0.7 %shard_map.84 = (f32[2,4,4,512]{3,2,1,0:T(4,128)}, f32[2,4,4,512]{3,2,1,0:T(4,128)}) custom-call(f32[64,4,128]{2,1,0:T(4,128)S(1)} %all_to_all.10.in_ref), custom_call_target="tpu_custom_call" | custom-call | flops 1000000 | bytes 500000 | tf_op jit(solution)/shard_map/pallas_call | solution.py:427
  (9 shorter events, 0.0 us)
Async XLA Ops:
  0.6 16.6 %copy-start = (f32[4,4,64,64]{3,2,1,0:T(8,128)S(1)}, f32[4,4,64,64]{3,2,1,0:T(8,128)}, u32[]{:S(2)}) copy-start(f32[4,4,64,64]{3,2,1,0:T(8,128)} %side_ref.1) | copy-start | bytes 786436
  2.4 14.8 %copy-start.1 = (f32[4,2,64,64]{3,2,1,0:T(8,128)S(1)}, f32[4,2,64,64]{3,2,1,0:T(8,128)}, u32[]{:S(2)}) copy-start(f32[4,2,64,64]{3,2,1,0:T(8,128)} %z_ref.1) | copy-start | bytes 393220
  2.4 14.8 %copy-start.2 = (f32[4,64,64]{2,1,0:T(8,128)S(1)}, f32[4,64,64]{2,1,0:T(8,128)}, u32[]{:S(2)}) copy-start(f32[4,64,64]{2,1,0:T(8,128)} %diag_ref.1) | copy-start | bytes 196612
  2.4 28.2 %all-to-all-start = ((f32[64,5,128]{2,1,0:T(8,128)}), f32[64,5,128]{2,1,0:T(8,128)S(1)}, u32[]{:S(2)}, u32[]{:S(2)}) async-start(f32[64,5,128]{2,1,0:T(8,128)} %shard_map.77), calls=%async_computation | async-start | bytes 524288 | tf_op jit(solution)/shard_map/all_to_all | solution.py:383
  30.8 6.1 %collective-permute-start.3 = (f32[128,128]{1,0:T(8,128)S(1)}, f32[128,128]{1,0:T(8,128)S(1)}, u32[]{:S(2)}, u32[]{:S(2)}) collective-permute-start(f32[128,128]{1,0:T(8,128)S(1)} %get-tuple-element.14.after_ref.start_ref), channel_id=1, source_target_pairs={{0,2},{8,0},{16,8},{24,16},{26,24},{18,26},{10,18},{2,10},{1,3},{9... | collective-permute-start | bytes 196616 | tf_op jit(solution)/shard_map/ppermute | solution.py:353
  32.3 4.6 %collective-permute-start.2 = (f32[128,128]{1,0:T(8,128)S(1)}, f32[128,128]{1,0:T(8,128)S(1)}, u32[]{:S(2)}, u32[]{:S(2)}) collective-permute-start(f32[128,128]{1,0:T(8,128)S(1)} %get-tuple-element.14.after_ref.start_ref), channel_id=1, source_target_pairs={{0,8},{8,16},{16,24},{24,26},{26,18},{18,10},{10,2},{2,0},{1,9},{9... | collective-permute-start | bytes 196616 | tf_op jit(solution)/shard_map/ppermute | solution.py:353
  32.8 4.3 %collective-permute-start.1 = (f32[128,128]{1,0:T(8,128)S(1)}, f32[128,128]{1,0:T(8,128)S(1)}, u32[]{:S(2)}, u32[]{:S(2)}) collective-permute-start(f32[128,128]{1,0:T(8,128)S(1)} %get-tuple-element.14.after_ref.start_ref), channel_id=1, source_target_pairs={{0,1},{32,0},{64,32},{96,64},{97,96},{65,97},{33,65},{1,33},{2,3},... | collective-permute-start | bytes 196616 | tf_op jit(solution)/shard_map/ppermute | solution.py:353
  33.5 4.3 %collective-permute-start = (f32[128,128]{1,0:T(8,128)S(1)}, f32[128,128]{1,0:T(8,128)S(1)}, u32[]{:S(2)}, u32[]{:S(2)}) collective-permute-start(f32[128,128]{1,0:T(8,128)S(1)} %get-tuple-element.14.after_ref.start_ref), channel_id=1, source_target_pairs={{0,32},{32,64},{64,96},{96,97},{97,65},{65,33},{33,1},{1,0},{2,34}... | collective-permute-start | bytes 196616 | tf_op jit(solution)/shard_map/ppermute | solution.py:353
  40.9 6.0 %collective-permute-start.7 = (f32[128,128]{1,0:T(8,128)S(1)}, f32[128,128]{1,0:T(8,128)S(1)}, u32[]{:S(2)}, u32[]{:S(2)}) collective-permute-start(f32[128,128]{1,0:T(8,128)S(1)} %get-tuple-element.22.after_ref.forward_ref), channel_id=1, source_target_pairs={{0,2},{8,0},{16,8},{24,16},{26,24},{18,26},{10,18},{2,10},{1,3},{9... | collective-permute-start | bytes 196616 | tf_op jit(solution)/shard_map/ppermute | solution.py:353
  42.4 4.5 %collective-permute-start.6 = (f32[128,128]{1,0:T(8,128)S(1)}, f32[128,128]{1,0:T(8,128)S(1)}, u32[]{:S(2)}, u32[]{:S(2)}) collective-permute-start(f32[128,128]{1,0:T(8,128)S(1)} %get-tuple-element.22.after_ref.forward_ref), channel_id=1, source_target_pairs={{0,8},{8,16},{16,24},{24,26},{26,18},{18,10},{10,2},{2,0},{1,9},{9... | collective-permute-start | bytes 196616 | tf_op jit(solution)/shard_map/ppermute | solution.py:353
  42.9 4.3 %collective-permute-start.5 = (f32[128,128]{1,0:T(8,128)S(1)}, f32[128,128]{1,0:T(8,128)S(1)}, u32[]{:S(2)}, u32[]{:S(2)}) collective-permute-start(f32[128,128]{1,0:T(8,128)S(1)} %get-tuple-element.22.after_ref.forward_ref), channel_id=1, source_target_pairs={{0,1},{32,0},{64,32},{96,64},{97,96},{65,97},{33,65},{1,33},{2,3},... | collective-permute-start | bytes 196616 | tf_op jit(solution)/shard_map/ppermute | solution.py:353
  44.3 4.3 %collective-permute-start.4 = (f32[128,128]{1,0:T(8,128)S(1)}, f32[128,128]{1,0:T(8,128)S(1)}, u32[]{:S(2)}, u32[]{:S(2)}) collective-permute-start(f32[128,128]{1,0:T(8,128)S(1)} %get-tuple-element.22.after_ref.forward_ref), channel_id=1, source_target_pairs={{0,32},{32,64},{64,96},{96,97},{97,65},{65,33},{33,1},{1,0},{2,34}... | collective-permute-start | bytes 196616 | tf_op jit(solution)/shard_map/ppermute | solution.py:353

commit v5 on v4

--- a/solution.py
+++ b/solution.py
@@ -226,18 +226,25 @@
     lane = lax.broadcasted_iota(jnp.int32, (DOFS, LANES), 1)
     low = lane < DOFS
     unit = jnp.where((lane & (DOFS - 1)) == row, 1.0, 0.0)
+    tiles = (DOFS // 8, 8, LANES)
     upright = jnp.zeros((DOFS, LANES), F32)
+    standing = {}
     for place, chunk in enumerate(chunks):
         end = ends_ref[chunk : chunk + 1, :]
         if place % 2 == 0:
-            heads_ref[chunk : chunk + 1, :] = jnp.sum(upright * unit, axis=0, keepdims=True)
-            flat = jnp.sum(upright * map_ref[chunk], axis=0, keepdims=True) + end
+            standing[chunk] = jnp.sum((upright * unit).reshape(tiles), axis=0)
+            flat = jnp.sum((upright * map_ref[chunk]).reshape(tiles), axis=0)
+            for distance in (4, 2, 1):
+                flat = flat + pltpu.roll(flat, distance, 0)
+            flat = flat + end
         else:
-            heads_ref[chunk : chunk + 1, :] = flat
-            terms = flat * map_ref[chunk] + end * unit
+            heads_ref[chunk : chunk + 1, :] = flat[0:1]
+            terms = (flat[None] * map_ref[chunk].reshape(tiles)).reshape(DOFS, LANES) + end * unit
             first = jnp.sum(jnp.where(low, terms, 0.0), axis=1, keepdims=True)
             second = jnp.sum(jnp.where(low, 0.0, terms), axis=1, keepdims=True)
             upright = jnp.where(low, first, second)
+    for chunk, parts in standing.items():
+        heads_ref[chunk : chunk + 1, :] = jnp.sum(parts, axis=0, keepdims=True)
 
     state = doubled(heads_ref[...])
     for step in steps:

time: 70.8 us -> 70.7 us (level)
  no operation moved by 1% of the time
where the time goes in v5:
time: 70.7 us; the launch traced here: 70.5 us
  starting transfers between devices  22.9 us (32%)
  blocking collectives  18.2 us (26%)
  waiting for transfers between devices  15 us (21%)
  Pallas kernels  13.6 us (19%)
  between operations  0.78 us (1%)
    all_to_all x1, blocking collectives, per_device(): returned = lax.all_to_all(ready, GZ, 0, 0, tiled=True)  18.2 us
    all_to_all x1, starting transfers between devices, per_device(): arrived = lax.all_to_all(packed, GZ, 0, 0, tiled=True)  14.8 us
    all_to_all x1, waiting for transfers between devices, per_device(): arrived = lax.all_to_all(packed, GZ, 0, 0, tiled=True)  12.5 us
    ppermute x8, starting transfers between devices, moved(): return lax.ppermute(value, axes, pairs)  8.13 us
    pallas_call x2, Pallas kernels, maps(): call(functools.partial(maps_kernel, q), shape(CHUNKS, DOFS, LANES), [VMEM...  3.98 us
    pallas_call x1, Pallas kernels, per_device(): call(forward_kernel, (field, shape(STEPS, 2 * CHUNKS, LANES)), [VMEM] * 1...  3.06 us
    pallas_call x1, Pallas kernels, per_device(): call(backward_kernel, shape(PEERS, 4, LANES), [VMEM] * 11, chain_scratch...  3.06 us
    ppermute x8, waiting for transfers between devices, moved(): return lax.ppermute(value, axes, pairs)  2.48 us
  transfers between devices with their start and end apart: 9, of which 5 were waited for; matrix products, arithmetic and copies ran while one was open for 0% of the time, Pallas kernels for 7%

profile of v5, /device:TPU:2, one launch (start us, length us, event | category | flops | bytes accessed | tf_op | source)
XLA Modules:
  0.0 70.5 jit_solution(3936231909127256237)
XLA Ops:
  0.6 1.8 %shard_map.77 = f32[64,5,128]{2,1,0:T(8,128)} custom-call(s32[2,4,4]{2,1,0:T(4,128)} %mat_hbm.1, f32[2,4,4,512]{3,2,1,0:T(4,128)} %rhs_hbm.1, f32[2,4,4,512]{3,2,1,0:T(4,128)} %start_hbm.1), custom_call_target="tpu_custom_call" | custom-call | flops 1000000 | bytes 500000 | tf_op jit(solution)/shard_map/pallas_call | solution.py:375
  2.4 0.0 copy-start.2
  2.4 14.8 %all-to-all-start = ((f32[64,5,128]{2,1,0:T(8,128)}), f32[64,5,128]{2,1,0:T(8,128)S(1)}, u32[]{:S(2)}, u32[]{:S(2)}) async-start(f32[64,5,128]{2,1,0:T(8,128)} %shard_map.77), calls=%async_computation | async-start | bytes 524288 | tf_op jit(solution)/shard_map/all_to_all | solution.py:390
  17.3 0.9 %shard_map.79 = (bf16[2,256,256]{2,1,0:T(8,128)(2,1)S(1)}, bf16[2,256,256]{2,1,0:T(8,128)(2,1)S(1)}, bf16[2,128,256]{2,1,0:T(8,128)(2,1)S(1)}, f32[2,4,64,128]{3,2,1,0:T(8,128)S(1)}) custom-call(f32[4,64,64]{2,1,0:T(8,128)S(1)} %copy-done.2, f32[4,2,64,64]{3,2,1,0:T(8,128)S(1)} %copy-done.1, f32[4,4,64,64]{3,2,1,0:T(8,128)S(1)} %copy-done), custom_call_target="tpu_custom_call" | custom-call | flops 4000000000 | bytes 500000 | tf_op jit(solution)/shard_map/pallas_call | solution.py:392
  18.1 12.5 %all-to-all-done.in_ref = f32[64,5,128]{2,1,0:T(8,128)S(1)} async-done(((f32[64,5,128]{2,1,0:T(8,128)}), f32[64,5,128]{2,1,0:T(8,128)S(1)}, u32[]{:S(2)}, u32[]{:S(2)}) %all-to-all-start) | async-done | bytes 163872 | tf_op jit(solution)/shard_map/all_to_all | solution.py:390
  30.6 0.1 shard_map.78
  30.8 1.5 %collective-permute-start.3 = (f32[128,128]{1,0:T(8,128)S(1)}, f32[128,128]{1,0:T(8,128)S(1)}, u32[]{:S(2)}, u32[]{:S(2)}) collective-permute-start(f32[128,128]{1,0:T(8,128)S(1)} %get-tuple-element.14.after_ref.start_ref), channel_id=1, source_target_pairs={{0,2},{8,0},{16,8},{24,16},{26,24},{18,26},{10,18},{2,10},{1,3},{9... | collective-permute-start | bytes 196616 | tf_op jit(solution)/shard_map/ppermute | solution.py:360
  32.3 0.5 collective-permute-start.2
  32.8 0.7 collective-permute-start.1
  33.5 1.4 %collective-permute-start = (f32[128,128]{1,0:T(8,128)S(1)}, f32[128,128]{1,0:T(8,128)S(1)}, u32[]{:S(2)}, u32[]{:S(2)}) collective-permute-start(f32[128,128]{1,0:T(8,128)S(1)} %get-tuple-element.14.after_ref.start_ref), channel_id=1, source_target_pairs={{0,32},{32,64},{64,96},{96,97},{97,65},{65,33},{33,1},{1,0},{2,34}... | collective-permute-start | bytes 196616 | tf_op jit(solution)/shard_map/ppermute | solution.py:360
  34.9 2.0 %shard_map.80.map_ref = f32[32,64,128]{2,1,0:T(8,128)S(1)} custom-call(f32[128,128]{1,0:T(8,128)S(1)} %get-tuple-element.20.kind_ref, bf16[128,128]{1,0:T(8,128)(2,1)S(1)} %get-tuple-element.15.mask_a_ref, bf16[128,128]{1,0:T(8,128)(2,1)S(1)} %get-tuple-element.16.mask_b_ref, bf16[2,256,256]{2,1,0:T(8,128)(2,1)S(1)} %get-tuple-element.17.tables_ref, ...), custom_call_target="tpu_custom_call" | custom-call | flops 4000000000 | bytes 500000 | tf_op jit(solution)/shard_map/pallas_call | solution.py:402
  36.9 0.2 collective-permute-done.1.n1_ref
  37.1 0.7 collective-permute-done.n0_ref
  37.8 3.1 %shard_map.81 = (f32[128,128]{1,0:T(8,128)S(1)}, f32[4,64,128]{2,1,0:T(8,128)S(1)}) custom-call(f32[128,128]{1,0:T(8,128)S(1)} %get-tuple-element.13.rhs_ref, f32[128,128]{1,0:T(8,128)S(1)} %get-tuple-element.14.after_ref.start_ref, f32[128,128]{1,0:T(8,128)S(1)} %collective-permute-done.n0_ref, f32[128,128]{1,0:T(8,128)S(1)} %collective-permute-done.1.n1_ref, ...), custom_call_target="tpu_custom_call" | custom-call | flops 4000000000 | bytes 500000 | tf_op jit(solution)/shard_map/pallas_call | solution.py:415
  40.8 1.5 %collective-permute-start.7 = (f32[128,128]{1,0:T(8,128)S(1)}, f32[128,128]{1,0:T(8,128)S(1)}, u32[]{:S(2)}, u32[]{:S(2)}) collective-permute-start(f32[128,128]{1,0:T(8,128)S(1)} %get-tuple-element.22.after_ref.forward_ref), channel_id=1, source_target_pairs={{0,2},{8,0},{16,8},{24,16},{26,24},{18,26},{10,18},{2,10},{1,3},{9... | collective-permute-start | bytes 196616 | tf_op jit(solution)/shard_map/ppermute | solution.py:360
  42.4 0.5 collective-permute-start.6
  42.9 1.3 %collective-permute-start.5 = (f32[128,128]{1,0:T(8,128)S(1)}, f32[128,128]{1,0:T(8,128)S(1)}, u32[]{:S(2)}, u32[]{:S(2)}) collective-permute-start(f32[128,128]{1,0:T(8,128)S(1)} %get-tuple-element.22.after_ref.forward_ref), channel_id=1, source_target_pairs={{0,1},{32,0},{64,32},{96,64},{97,96},{65,97},{33,65},{1,33},{2,3},... | collective-permute-start | bytes 196616 | tf_op jit(solution)/shard_map/ppermute | solution.py:360
  44.2 0.7 collective-permute-start.4
  44.9 2.0 %shard_map.82.map_ref = f32[32,64,128]{2,1,0:T(8,128)S(1)} custom-call(f32[128,128]{1,0:T(8,128)S(1)} %get-tuple-element.20.kind_ref, bf16[128,128]{1,0:T(8,128)(2,1)S(1)} %get-tuple-element.15.mask_a_ref, bf16[128,128]{1,0:T(8,128)(2,1)S(1)} %get-tuple-element.16.mask_b_ref, bf16[2,256,256]{2,1,0:T(8,128)(2,1)S(1)} %get-tuple-element.17.tables_ref, ...), custom_call_target="tpu_custom_call" | custom-call | flops 4000000000 | bytes 500000 | tf_op jit(solution)/shard_map/pallas_call | solution.py:402
  46.9 0.3 collective-permute-done.5.n1_ref
  47.2 1.3 %collective-permute-done.4.n0_ref = f32[128,128]{1,0:T(8,128)S(1)} collective-permute-done((f32[128,128]{1,0:T(8,128)S(1)}, f32[128,128]{1,0:T(8,128)S(1)}, u32[]{:S(2)}, u32[]{:S(2)}) %collective-permute-start.4) | collective-permute-done | bytes 65568 | tf_op jit(solution)/shard_map/ppermute | solution.py:360
  48.5 3.1 %shard_map.83 = f32[64,4,128]{2,1,0:T(4,128)S(1)} custom-call(f32[128,128]{1,0:T(8,128)S(1)} %get-tuple-element.22.after_ref.forward_ref, f32[4,64,128]{2,1,0:T(8,128)S(1)} %get-tuple-element.23.given_ref, f32[128,128]{1,0:T(8,128)S(1)} %collective-permute-done.4.n0_ref, f32[128,128]{1,0:T(8,128)S(1)} %collective-permute-done.5.n1_ref, ...), custom_call_target="tpu_custom_call" | custom-call | flops 4000000000 | bytes 500000 | tf_op jit(solution)/shard_map/pallas_call | solution.py:425
  51.6 18.2 %all_to_all.10.in_ref = f32[64,4,128]{2,1,0:T(4,128)S(1)} all-to-all(f32[64,4,128]{2,1,0:T(4,128)S(1)} %shard_map.83), channel_id=1, replica_groups=mesh['ah'=2,'am'=2,'al'=2,'b'=4,'c'=2,'gx'=2,'gy'=2] {'ah','am','al','b'..., dimensions={0} | all-to-all | bytes 262144 | tf_op jit(solution)/shard_map/all_to_all | solution.py:432
  69.8 0.7 %shard_map.84 = (f32[2,4,4,512]{3,2,1,0:T(4,128)}, f32[2,4,4,512]{3,2,1,0:T(4,128)}) custom-call(f32[64,4,128]{2,1,0:T(4,128)S(1)} %all_to_all.10.in_ref), custom_call_target="tpu_custom_call" | custom-call | flops 1000000 | bytes 500000 | tf_op jit(solution)/shard_map/pallas_call | solution.py:434
  (9 shorter events, 0.0 us)
Async XLA Ops:
  0.6 16.6 %copy-start = (f32[4,4,64,64]{3,2,1,0:T(8,128)S(1)}, f32[4,4,64,64]{3,2,1,0:T(8,128)}, u32[]{:S(2)}) copy-start(f32[4,4,64,64]{3,2,1,0:T(8,128)} %side_ref.1) | copy-start | bytes 786436
  2.4 14.8 %copy-start.1 = (f32[4,2,64,64]{3,2,1,0:T(8,128)S(1)}, f32[4,2,64,64]{3,2,1,0:T(8,128)}, u32[]{:S(2)}) copy-start(f32[4,2,64,64]{3,2,1,0:T(8,128)} %z_ref.1) | copy-start | bytes 393220
  2.4 14.8 %copy-start.2 = (f32[4,64,64]{2,1,0:T(8,128)S(1)}, f32[4,64,64]{2,1,0:T(8,128)}, u32[]{:S(2)}) copy-start(f32[4,64,64]{2,1,0:T(8,128)} %diag_ref.1) | copy-start | bytes 196612
  2.4 28.2 %all-to-all-start = ((f32[64,5,128]{2,1,0:T(8,128)}), f32[64,5,128]{2,1,0:T(8,128)S(1)}, u32[]{:S(2)}, u32[]{:S(2)}) async-start(f32[64,5,128]{2,1,0:T(8,128)} %shard_map.77), calls=%async_computation | async-start | bytes 524288 | tf_op jit(solution)/shard_map/all_to_all | solution.py:390
  30.8 6.1 %collective-permute-start.3 = (f32[128,128]{1,0:T(8,128)S(1)}, f32[128,128]{1,0:T(8,128)S(1)}, u32[]{:S(2)}, u32[]{:S(2)}) collective-permute-start(f32[128,128]{1,0:T(8,128)S(1)} %get-tuple-element.14.after_ref.start_ref), channel_id=1, source_target_pairs={{0,2},{8,0},{16,8},{24,16},{26,24},{18,26},{10,18},{2,10},{1,3},{9... | collective-permute-start | bytes 196616 | tf_op jit(solution)/shard_map/ppermute | solution.py:360
  32.3 4.6 %collective-permute-start.2 = (f32[128,128]{1,0:T(8,128)S(1)}, f32[128,128]{1,0:T(8,128)S(1)}, u32[]{:S(2)}, u32[]{:S(2)}) collective-permute-start(f32[128,128]{1,0:T(8,128)S(1)} %get-tuple-element.14.after_ref.start_ref), channel_id=1, source_target_pairs={{0,8},{8,16},{16,24},{24,26},{26,18},{18,10},{10,2},{2,0},{1,9},{9... | collective-permute-start | bytes 196616 | tf_op jit(solution)/shard_map/ppermute | solution.py:360
  32.8 4.3 %collective-permute-start.1 = (f32[128,128]{1,0:T(8,128)S(1)}, f32[128,128]{1,0:T(8,128)S(1)}, u32[]{:S(2)}, u32[]{:S(2)}) collective-permute-start(f32[128,128]{1,0:T(8,128)S(1)} %get-tuple-element.14.after_ref.start_ref), channel_id=1, source_target_pairs={{0,1},{32,0},{64,32},{96,64},{97,96},{65,97},{33,65},{1,33},{2,3},... | collective-permute-start | bytes 196616 | tf_op jit(solution)/shard_map/ppermute | solution.py:360
  33.5 4.3 %collective-permute-start = (f32[128,128]{1,0:T(8,128)S(1)}, f32[128,128]{1,0:T(8,128)S(1)}, u32[]{:S(2)}, u32[]{:S(2)}) collective-permute-start(f32[128,128]{1,0:T(8,128)S(1)} %get-tuple-element.14.after_ref.start_ref), channel_id=1, source_target_pairs={{0,32},{32,64},{64,96},{96,97},{97,65},{65,33},{33,1},{1,0},{2,34}... | collective-permute-start | bytes 196616 | tf_op jit(solution)/shard_map/ppermute | solution.py:360
  40.8 6.0 %collective-permute-start.7 = (f32[128,128]{1,0:T(8,128)S(1)}, f32[128,128]{1,0:T(8,128)S(1)}, u32[]{:S(2)}, u32[]{:S(2)}) collective-permute-start(f32[128,128]{1,0:T(8,128)S(1)} %get-tuple-element.22.after_ref.forward_ref), channel_id=1, source_target_pairs={{0,2},{8,0},{16,8},{24,16},{26,24},{18,26},{10,18},{2,10},{1,3},{9... | collective-permute-start | bytes 196616 | tf_op jit(solution)/shard_map/ppermute | solution.py:360
  42.4 4.5 %collective-permute-start.6 = (f32[128,128]{1,0:T(8,128)S(1)}, f32[128,128]{1,0:T(8,128)S(1)}, u32[]{:S(2)}, u32[]{:S(2)}) collective-permute-start(f32[128,128]{1,0:T(8,128)S(1)} %get-tuple-element.22.after_ref.forward_ref), channel_id=1, source_target_pairs={{0,8},{8,16},{16,24},{24,26},{26,18},{18,10},{10,2},{2,0},{1,9},{9... | collective-permute-start | bytes 196616 | tf_op jit(solution)/shard_map/ppermute | solution.py:360
  42.9 4.3 %collective-permute-start.5 = (f32[128,128]{1,0:T(8,128)S(1)}, f32[128,128]{1,0:T(8,128)S(1)}, u32[]{:S(2)}, u32[]{:S(2)}) collective-permute-start(f32[128,128]{1,0:T(8,128)S(1)} %get-tuple-element.22.after_ref.forward_ref), channel_id=1, source_target_pairs={{0,1},{32,0},{64,32},{96,64},{97,96},{65,97},{33,65},{1,33},{2,3},... | collective-permute-start | bytes 196616 | tf_op jit(solution)/shard_map/ppermute | solution.py:360
  44.2 4.3 %collective-permute-start.4 = (f32[128,128]{1,0:T(8,128)S(1)}, f32[128,128]{1,0:T(8,128)S(1)}, u32[]{:S(2)}, u32[]{:S(2)}) collective-permute-start(f32[128,128]{1,0:T(8,128)S(1)} %get-tuple-element.22.after_ref.forward_ref), channel_id=1, source_target_pairs={{0,32},{32,64},{64,96},{96,97},{97,65},{65,33},{33,1},{1,0},{2,34}... | collective-permute-start | bytes 196616 | tf_op jit(solution)/shard_map/ppermute | solution.py:360
